TPU v7x, 32 devices: a whole 2x2x4 slice. The times are simulated.
32 devices in a mesh: grp: 2 (over x), col: 16 (over z, y, core).
Axes of the slice: x: 2, y: 2, z: 4, core: 2. Of those that a mesh axis runs over, the one named last changes fastest.
Arguments:
- leaf_right_hand: float32 [320, 256, 128], P(('grp', 'col')), parts along dimension 0, may hold values from -6 to 6
- leaf_diagonal_inverse: bfloat16 [320, 256, 256], P(('grp', 'col')), parts along dimension 0, as said below
- leaf_coupling: bfloat16 [320, 4, 256, 256], P(('grp', 'col')), parts along dimension 0, may hold values from -0.03125 to 0.03125
- leaf_pattern: int32 [320, 4], P(('grp', 'col')), parts along dimension 0, may hold values 0 or 1
- top_rhs: float32 [32, 256, 128], P(('grp', 'col')), parts along dimension 0, may hold values from -6 to 6
- top_inverse: bfloat16 [32, 256, 256], P(('grp', 'col')), parts along dimension 0, as said below
- top_coupling: bfloat16 [32, 4, 256, 256], P(('grp', 'col')), parts along dimension 0, may hold values from -0.09375 to 0.09375
Outputs:
- leaf_solution: float32 [320, 256, 128], P(('grp', 'col')), parts along dimension 0
- top_solution: float32 [32, 256, 128], P(('grp', 'col')), parts along dimension 0
There are 2 independent parts, one for each index of `grp`. A program takes and returns all parts, laid end to end along the dimension named above; each array names one. Nothing has to cross between parts.
Inputs may be any that keep to these rules, and one draw needn't show every extreme that they name: `leaf_diagonal_inverse`: lower triangular, diagonal between 0.7 and 1.3. `top_inverse`: lower triangular, diagonal between 0.7 and 1.3.
All inputs are finite; a program needn't handle non-finite values. No bound on the sum of `leaf_pattern` on one device may be relied on, other than what follows from the above.
Results may differ from a plain program's by a relative error of at most 0.0044.
Values sent between devices are 32-bit elements; how exact they have to be, the bound alone decides.
No kernel may reach another device: no remote copies, remote signals or barrier semaphores. Data moves between devices by JAX's collectives and lax.ppermute only.
A program may use at most 64 MiB of HBM per device.

v0:
```python
import jax
import jax.numpy as jnp
from jax import lax
from jax.sharding import PartitionSpec as P


def from_partner(shard, axis, distance):
    return lax.ppermute(shard, axis, [(i, i ^ 1 << distance) for i in range(lax.axis_size(axis))])


def rounded_result(value):
    return value.astype(jnp.bfloat16)


def local(
    leaf_right_hand,
    leaf_diagonal_inverse,
    leaf_coupling,
    leaf_pattern,
    top_rhs,
    top_inverse,
    top_coupling,
):
    count = lax.axis_size("col")
    depth = count.bit_length() - 1
    device = lax.axis_index("col")
    bit_values = device >> jnp.arange(depth, dtype=jnp.int32) & 1
    trailing = jnp.sum(jnp.cumprod(bit_values))
    own_level = depth - 1 - trailing
    mask_values = leaf_pattern.astype(jnp.bfloat16)[:, :, None, None]
    leaf_forward = jnp.einsum(
        "efj,ejs->efs",
        leaf_diagonal_inverse,
        rounded_result(leaf_right_hand),
        preferred_element_type=jnp.float32,
    )
    masked = mask_values * rounded_result(leaf_forward)[:, None]
    leaf_terms = jnp.einsum(
        "ikab,ikbr->kar", leaf_coupling, masked, preferred_element_type=jnp.float32
    )
    inverse_own = top_inverse[0]
    coupling_own = top_coupling[0]
    rhs_own = top_rhs[0]
    zeros_block = jnp.zeros_like(rhs_own)
    forward_own = zeros_block
    partial_terms = leaf_terms
    for level in reversed(range(depth)):
        total = partial_terms[level]
        for bit in range(depth - level):
            total = total + from_partner(total, "col", bit)
        owner_here = own_level == level
        solved = jnp.dot(
            inverse_own, rounded_result(rhs_own - total), preferred_element_type=jnp.float32
        )
        forward_own = jnp.where(owner_here, solved, forward_own)
        if level > 0:
            upward = jnp.einsum(
                "kab,br->kar",
                coupling_own[:level],
                rounded_result(solved),
                preferred_element_type=jnp.float32,
            )
            partial_terms = partial_terms[:level] + jnp.where(owner_here, upward, 0.0)
    backward_own = zeros_block
    columns = []
    for level in range(depth):
        owner_here = own_level == level
        carried_value = zeros_block
        if level > 0:
            known = jnp.stack(columns)
            carried_value = jnp.einsum(
                "kab,kar->br",
                coupling_own[:level],
                rounded_result(known),
                preferred_element_type=jnp.float32,
            )
        solved = jnp.einsum(
            "ab,ar->br",
            inverse_own,
            rounded_result(forward_own - carried_value),
            preferred_element_type=jnp.float32,
        )
        backward_own = jnp.where(owner_here, solved, backward_own)
        spread_value = jnp.where(owner_here, solved, 0.0)
        for bit in range(depth - level):
            spread_value = spread_value + from_partner(spread_value, "col", bit)
        columns.append(spread_value)
    path_values = jnp.stack(columns)
    masked_path = mask_values * rounded_result(path_values)[None]
    carried_leaf = jnp.einsum(
        "ikab,ikar->ibr", leaf_coupling, masked_path, preferred_element_type=jnp.float32
    )
    leaf_solution = jnp.einsum(
        "vdu,vdo->vuo",
        leaf_diagonal_inverse,
        rounded_result(leaf_forward - carried_leaf),
        preferred_element_type=jnp.float32,
    )
    top_out = jnp.where(own_level >= 0, backward_own, path_values[0])[None]
    return (leaf_solution, top_out)


def solution(mesh):
    in_specs = (
        P(("grp", "col"), None, None),
        P(("grp", "col"), None, None),
        P(("grp", "col"), None, None, None),
        P(("grp", "col"), None),
        P(("grp", "col"), None, None),
        P(("grp", "col"), None, None),
        P(("grp", "col"), None, None, None),
    )
    out_specs = (P(("grp", "col"), None, None), P(("grp", "col"), None, None))
    return jax.shard_map(local, mesh=mesh, in_specs=in_specs, out_specs=out_specs, check_vma=False)
```

profile of v0, /device:TPU:0, one launch (start us, length us, event | category | flops | bytes accessed | tf_op | source)
XLA Modules:
  0.0 100.9 jit_solution(17437780608173122712)
XLA Ops:
  0.6 0.0 copy-start
  0.6 0.8 convert_element_type.60
  1.4 0.5 copy-done
  2.0 2.9 %fusion.119 = (bf16[10,256,128]{2,1,0:T(8,128)(2,1)S(1)}, f32[10,256,128]{2,1,0:T(8,128)}) fusion(bf16[10,256,256]{2,1,0:T(8,128)(2,1)S(1)} %copy-done, f32[10,256,128]{2,1,0:T(8,128)} %param.7), kind=kOutput, calls=%fused_computation.107 | convolution fusion | flops 168427520 | bytes 4587520 | tf_op jit(solution)/shard_map/efj,ejs->efs/dot_general | solution.py:31
  4.8 0.3 copy.16
  5.1 0.0 copy-start.3
  5.1 0.0 copy-start.1
  5.1 4.4 %fusion.29 = f32[4,256,128]{1,2,0:T(8,128)S(1)} fusion(bf16[10,4,256,256]{3,2,1,0:T(8,128)(2,1)} %param.9, bf16[10,256,128]{1,2,0:T(8,128)(2,1)S(1)} %copy.16, bf16[10,4]{0,1:T(4,128)(2,1)S(1)} %convert_element_type.60), kind=kOutput, calls=%fused_computation.14 | convolution fusion | flops 672399360 | bytes 6422608 | tf_op jit(solution)/shard_map/ikab,ikbr->kar/dot_general | solution.py:38
  9.5 0.6 collective-permute-start
  10.1 0.2 reduce-window.6
  10.3 0.6 reduce_sum.9
  11.6 0.1 copy.15
  11.7 0.2 fusion.89
  11.9 0.3 fusion.35
  12.2 0.1 collective-permute-start.1
  12.3 1.3 %collective-permute-done.1 = f32[256,128]{0,1:T(8,128)S(1)} collective-permute-done((f32[256,128]{0,1:T(8,128)S(1)}, f32[256,128]{0,1:T(8,128)S(1)}, u32[]{:S(2)}, u32[]{:S(2)}) %collective-permute-start.1) | collective-permute-done | bytes 131104 | tf_op jit(solution)/shard_map/ppermute | solution.py:8
  13.6 2.7 %collective-permute-start.2 = (f32[256,128]{0,1:T(8,128)S(1)}, f32[256,128]{0,1:T(8,128)S(1)}, u32[]{:S(2)}, u32[]{:S(2)}) collective-permute-start(f32[256,128]{0,1:T(8,128)S(1)} %fusion.117), channel_id=1, source_target_pairs={{0,2},{1,3},{2,0},{3,1},{4,6},{5,7},{6,4},{7,5},{8,10},{9,11},{10,... | collective-permute-start | bytes 393224 | tf_op jit(solution)/shard_map/ppermute | solution.py:8
  16.4 4.0 %collective-permute-done.2 = f32[256,128]{0,1:T(8,128)S(1)} collective-permute-done((f32[256,128]{0,1:T(8,128)S(1)}, f32[256,128]{0,1:T(8,128)S(1)}, u32[]{:S(2)}, u32[]{:S(2)}) %collective-permute-start.2) | collective-permute-done | bytes 131104 | tf_op jit(solution)/shard_map/ppermute | solution.py:8
  20.4 0.2 fusion.87
  20.6 0.2 fusion.37
  20.8 0.1 collective-permute-start.3
  20.9 1.3 %collective-permute-done.3 = f32[256,128]{0,1:T(8,128)S(1)} collective-permute-done((f32[256,128]{0,1:T(8,128)S(1)}, f32[256,128]{0,1:T(8,128)S(1)}, u32[]{:S(2)}, u32[]{:S(2)}) %collective-permute-start.3) | collective-permute-done | bytes 131104 | tf_op jit(solution)/shard_map/ppermute | solution.py:8
  22.3 1.8 %collective-permute-start.4 = (f32[256,128]{0,1:T(8,128)S(1)}, f32[256,128]{0,1:T(8,128)S(1)}, u32[]{:S(2)}, u32[]{:S(2)}) collective-permute-start(f32[256,128]{0,1:T(8,128)S(1)} %fusion.118), channel_id=1, source_target_pairs={{0,2},{1,3},{2,0},{3,1},{4,6},{5,7},{6,4},{7,5},{8,10},{9,11},{10,... | collective-permute-start | bytes 393224 | tf_op jit(solution)/shard_map/ppermute | solution.py:8
  24.1 3.8 %collective-permute-done.4 = f32[256,128]{0,1:T(8,128)S(1)} collective-permute-done((f32[256,128]{0,1:T(8,128)S(1)}, f32[256,128]{0,1:T(8,128)S(1)}, u32[]{:S(2)}, u32[]{:S(2)}) %collective-permute-start.4) | collective-permute-done | bytes 131104 | tf_op jit(solution)/shard_map/ppermute | solution.py:8
  27.9 1.9 %collective-permute-start.5 = (f32[256,128]{0,1:T(8,128)S(1)}, f32[256,128]{0,1:T(8,128)S(1)}, u32[]{:S(2)}, u32[]{:S(2)}) collective-permute-start(f32[256,128]{0,1:T(8,128)S(1)} %add.75), channel_id=1, source_target_pairs={{0,4},{1,5},{2,6},{3,7},{4,0},{5,1},{6,2},{7,3},{8,12},{9,13},{10,... | collective-permute-start | bytes 393224 | tf_op jit(solution)/shard_map/ppermute | solution.py:8
  29.8 3.2 %collective-permute-done.5 = f32[256,128]{0,1:T(8,128)S(1)} collective-permute-done((f32[256,128]{0,1:T(8,128)S(1)}, f32[256,128]{0,1:T(8,128)S(1)}, u32[]{:S(2)}, u32[]{:S(2)}) %collective-permute-start.5) | collective-permute-done | bytes 131104 | tf_op jit(solution)/shard_map/ppermute | solution.py:8
  32.9 0.2 fusion.85
  33.1 0.2 fusion.41
  33.3 0.1 collective-permute-start.6
  33.4 1.3 %collective-permute-done.6 = f32[256,128]{0,1:T(8,128)S(1)} collective-permute-done((f32[256,128]{0,1:T(8,128)S(1)}, f32[256,128]{0,1:T(8,128)S(1)}, u32[]{:S(2)}, u32[]{:S(2)}) %collective-permute-start.6) | collective-permute-done | bytes 131104 | tf_op jit(solution)/shard_map/ppermute | solution.py:8
  34.8 1.8 %collective-permute-start.7 = (f32[256,128]{0,1:T(8,128)S(1)}, f32[256,128]{0,1:T(8,128)S(1)}, u32[]{:S(2)}, u32[]{:S(2)}) collective-permute-start(f32[256,128]{0,1:T(8,128)S(1)} %add.78), channel_id=1, source_target_pairs={{0,2},{1,3},{2,0},{3,1},{4,6},{5,7},{6,4},{7,5},{8,10},{9,11},{10,... | collective-permute-start | bytes 393224 | tf_op jit(solution)/shard_map/ppermute | solution.py:8
  36.6 3.8 %collective-permute-done.7 = f32[256,128]{0,1:T(8,128)S(1)} collective-permute-done((f32[256,128]{0,1:T(8,128)S(1)}, f32[256,128]{0,1:T(8,128)S(1)}, u32[]{:S(2)}, u32[]{:S(2)}) %collective-permute-start.7) | collective-permute-done | bytes 131104 | tf_op jit(solution)/shard_map/ppermute | solution.py:8
  40.4 1.9 %collective-permute-start.8 = (f32[256,128]{0,1:T(8,128)S(1)}, f32[256,128]{0,1:T(8,128)S(1)}, u32[]{:S(2)}, u32[]{:S(2)}) collective-permute-start(f32[256,128]{0,1:T(8,128)S(1)} %add.79), channel_id=1, source_target_pairs={{0,4},{1,5},{2,6},{3,7},{4,0},{5,1},{6,2},{7,3},{8,12},{9,13},{10,... | collective-permute-start | bytes 393224 | tf_op jit(solution)/shard_map/ppermute | solution.py:8
  42.3 3.2 %collective-permute-done.8 = f32[256,128]{0,1:T(8,128)S(1)} collective-permute-done((f32[256,128]{0,1:T(8,128)S(1)}, f32[256,128]{0,1:T(8,128)S(1)}, u32[]{:S(2)}, u32[]{:S(2)}) %collective-permute-start.8) | collective-permute-done | bytes 131104 | tf_op jit(solution)/shard_map/ppermute | solution.py:8
  45.5 2.9 %collective-permute-start.9 = (f32[256,128]{0,1:T(8,128)S(1)}, f32[256,128]{0,1:T(8,128)S(1)}, u32[]{:S(2)}, u32[]{:S(2)}) collective-permute-start(f32[256,128]{0,1:T(8,128)S(1)} %add.80), channel_id=1, source_target_pairs={{0,8},{1,9},{2,10},{3,11},{4,12},{5,13},{6,14},{7,15},{8,0},{9,1},... | collective-permute-start | bytes 393224 | tf_op jit(solution)/shard_map/ppermute | solution.py:8
  48.3 4.6 %collective-permute-done.9 = f32[256,128]{0,1:T(8,128)S(1)} collective-permute-done((f32[256,128]{0,1:T(8,128)S(1)}, f32[256,128]{0,1:T(8,128)S(1)}, u32[]{:S(2)}, u32[]{:S(2)}) %collective-permute-start.9) | collective-permute-done | bytes 131104 | tf_op jit(solution)/shard_map/ppermute | solution.py:8
  53.0 0.2 convolution_select_fusion.3
  53.2 0.2 fusion.38
  53.3 0.1 collective-permute-start.10
  53.4 1.3 %collective-permute-done.10 = f32[256,128]{0,1:T(8,128)S(1)} collective-permute-done((f32[256,128]{0,1:T(8,128)S(1)}, f32[256,128]{0,1:T(8,128)S(1)}, u32[]{:S(2)}, u32[]{:S(2)}) %collective-permute-start.10) | collective-permute-done | bytes 131104 | tf_op jit(solution)/shard_map/ppermute | solution.py:8
  54.8 1.6 %collective-permute-start.11 = (f32[256,128]{0,1:T(8,128)S(1)}, f32[256,128]{0,1:T(8,128)S(1)}, u32[]{:S(2)}, u32[]{:S(2)}) collective-permute-start(f32[256,128]{0,1:T(8,128)S(1)} %add.82), channel_id=1, source_target_pairs={{0,2},{1,3},{2,0},{3,1},{4,6},{5,7},{6,4},{7,5},{8,10},{9,11},{10,... | collective-permute-start | bytes 393224 | tf_op jit(solution)/shard_map/ppermute | solution.py:8
  56.4 4.0 %collective-permute-done.11 = f32[256,128]{0,1:T(8,128)S(1)} collective-permute-done((f32[256,128]{0,1:T(8,128)S(1)}, f32[256,128]{0,1:T(8,128)S(1)}, u32[]{:S(2)}, u32[]{:S(2)}) %collective-permute-start.11) | collective-permute-done | bytes 131104 | tf_op jit(solution)/shard_map/ppermute | solution.py:8
  60.4 0.8 collective-permute-start.12
  61.2 4.2 %collective-permute-done.12 = f32[256,128]{0,1:T(8,128)S(1)} collective-permute-done((f32[256,128]{0,1:T(8,128)S(1)}, f32[256,128]{0,1:T(8,128)S(1)}, u32[]{:S(2)}, u32[]{:S(2)}) %collective-permute-start.12) | collective-permute-done | bytes 131104 | tf_op jit(solution)/shard_map/ppermute | solution.py:8
  65.5 2.2 %collective-permute-start.13 = (f32[256,128]{0,1:T(8,128)S(1)}, f32[256,128]{0,1:T(8,128)S(1)}, u32[]{:S(2)}, u32[]{:S(2)}) collective-permute-start(f32[256,128]{0,1:T(8,128)S(1)} %add.84), channel_id=1, source_target_pairs={{0,8},{1,9},{2,10},{3,11},{4,12},{5,13},{6,14},{7,15},{8,0},{9,1},... | collective-permute-start | bytes 393224 | tf_op jit(solution)/shard_map/ppermute | solution.py:8
  67.6 5.2 %collective-permute-done.13 = f32[256,128]{0,1:T(8,128)S(1)} collective-permute-done((f32[256,128]{0,1:T(8,128)S(1)}, f32[256,128]{0,1:T(8,128)S(1)}, u32[]{:S(2)}, u32[]{:S(2)}) %collective-permute-start.13) | collective-permute-done | bytes 131104 | tf_op jit(solution)/shard_map/ppermute | solution.py:8
  72.8 0.3 broadcast_select_fusion.2
  73.1 0.1 collective-permute-start.14
  73.2 1.3 %collective-permute-done.14 = f32[256,128]{0,1:T(8,128)S(1)} collective-permute-done((f32[256,128]{0,1:T(8,128)S(1)}, f32[256,128]{0,1:T(8,128)S(1)}, u32[]{:S(2)}, u32[]{:S(2)}) %collective-permute-start.14) | collective-permute-done | bytes 131104 | tf_op jit(solution)/shard_map/ppermute | solution.py:8
  74.6 1.6 %collective-permute-start.15 = (f32[256,128]{0,1:T(8,128)S(1)}, f32[256,128]{0,1:T(8,128)S(1)}, u32[]{:S(2)}, u32[]{:S(2)}) collective-permute-start(f32[256,128]{0,1:T(8,128)S(1)} %add.86), channel_id=1, source_target_pairs={{0,2},{1,3},{2,0},{3,1},{4,6},{5,7},{6,4},{7,5},{8,10},{9,11},{10,... | collective-permute-start | bytes 393224 | tf_op jit(solution)/shard_map/ppermute | solution.py:8
  76.2 4.0 %collective-permute-done.15 = f32[256,128]{0,1:T(8,128)S(1)} collective-permute-done((f32[256,128]{0,1:T(8,128)S(1)}, f32[256,128]{0,1:T(8,128)S(1)}, u32[]{:S(2)}, u32[]{:S(2)}) %collective-permute-start.15) | collective-permute-done | bytes 131104 | tf_op jit(solution)/shard_map/ppermute | solution.py:8
  80.2 0.8 collective-permute-start.16
  81.0 4.3 %collective-permute-done.16 = f32[256,128]{0,1:T(8,128)S(1)} collective-permute-done((f32[256,128]{0,1:T(8,128)S(1)}, f32[256,128]{0,1:T(8,128)S(1)}, u32[]{:S(2)}, u32[]{:S(2)}) %collective-permute-start.16) | collective-permute-done | bytes 131104 | tf_op jit(solution)/shard_map/ppermute | solution.py:8
  85.3 0.3 broadcast_select_fusion.1
  85.6 0.1 collective-permute-start.17
  85.7 1.3 %collective-permute-done.17 = f32[256,128]{0,1:T(8,128)S(1)} collective-permute-done((f32[256,128]{0,1:T(8,128)S(1)}, f32[256,128]{0,1:T(8,128)S(1)}, u32[]{:S(2)}, u32[]{:S(2)}) %collective-permute-start.17) | collective-permute-done | bytes 131104 | tf_op jit(solution)/shard_map/ppermute | solution.py:8
  87.0 1.6 %collective-permute-start.18 = (f32[256,128]{0,1:T(8,128)S(1)}, f32[256,128]{0,1:T(8,128)S(1)}, u32[]{:S(2)}, u32[]{:S(2)}) collective-permute-start(f32[256,128]{0,1:T(8,128)S(1)} %add.89), channel_id=1, source_target_pairs={{0,2},{1,3},{2,0},{3,1},{4,6},{5,7},{6,4},{7,5},{8,10},{9,11},{10,... | collective-permute-start | bytes 393224 | tf_op jit(solution)/shard_map/ppermute | solution.py:8
  88.7 4.0 %collective-permute-done.18 = f32[256,128]{0,1:T(8,128)S(1)} collective-permute-done((f32[256,128]{0,1:T(8,128)S(1)}, f32[256,128]{0,1:T(8,128)S(1)}, u32[]{:S(2)}, u32[]{:S(2)}) %collective-permute-start.18) | collective-permute-done | bytes 131104 | tf_op jit(solution)/shard_map/ppermute | solution.py:8
  92.7 0.3 select_bitcast_fusion
  93.0 0.1 collective-permute-start.19
  93.1 0.8 copy.20
  93.9 0.6 collective-permute-done.19
  94.5 4.9 %convolution_bitcast_fusion = f32[10,256,128]{1,2,0:T(8,128)S(1)} fusion(bf16[10,256,256]{2,1,0:T(8,128)(2,1)S(1)} %copy-done, f32[10,256,128]{2,1,0:T(8,128)} %get-tuple-element.11, bf16[10,4,256,256]{3,2,1,0:T(8,128)(2,1)} %param.9, bf16[4,256,128]{1,2,0:T(8,128)(2,1)S(1)} %pad_maximum_fusion, bf16[10,4]{0,1:T(4,128)(2,1)S(1)} %convert_element_type.60), kind=kOutput, calls=%fused_computation.6 | convolution fusion | flops 840826880 | bytes 9437264 | tf_op jit(solution)/shard_map/vdu,vdo->vuo/dot_general | solution.py:93
  99.5 1.5 %copy.19 = f32[10,256,128]{2,1,0:T(8,128)} copy(f32[10,256,128]{1,2,0:T(8,128)S(1)} %convolution_bitcast_fusion) | data formatting | bytes 2621440
  (26 shorter events, 0.4 us)
Async XLA Ops:
  0.6 1.3 %copy-start = (bf16[10,256,256]{2,1,0:T(8,128)(2,1)S(1)}, bf16[10,256,256]{2,1,0:T(8,128)(2,1)}, u32[]{:S(2)}) copy-start(bf16[10,256,256]{2,1,0:T(8,128)(2,1)} %param.8) | copy-start | bytes 3932164
  5.1 6.5 %copy-start.3 = (f32[1,256,128]{2,1,0:T(8,128)S(1)}, f32[1,256,128]{2,1,0:T(8,128)}, u32[]{:S(2)}) copy-start(f32[1,256,128]{2,1,0:T(8,128)} %param.11) | copy-start | bytes 393220
  5.1 6.6 %copy-start.1 = (bf16[1,256,256]{2,1,0:T(8,128)(2,1)S(1)}, bf16[1,256,256]{2,1,0:T(8,128)(2,1)}, u32[]{:S(2)}) copy-start(bf16[1,256,256]{2,1,0:T(8,128)(2,1)} %param.12) | copy-start | bytes 393220
  9.5 2.4 %copy-start.2 = (bf16[1,4,256,256]{3,2,1,0:T(8,128)(2,1)S(1)}, bf16[1,4,256,256]{3,2,1,0:T(8,128)(2,1)}, u32[]{:S(2)}) copy-start(bf16[1,4,256,256]{3,2,1,0:T(8,128)(2,1)} %param.13) | copy-start | bytes 1572868
  9.5 2.2 %collective-permute-start = (f32[256,128]{0,1:T(8,128)S(1)}, f32[256,128]{0,1:T(8,128)S(1)}, u32[]{:S(2)}, u32[]{:S(2)}) collective-permute-start(f32[256,128]{0,1:T(8,128)S(1)} %slice_bitcast_fusion.2), channel_id=1, source_target_pairs={{0,1},{1,0},{2,3},{3,2},{4,5},{5,4},{6,7},{7,6},{8,9},{9,8},{10,11... | collective-permute-start | bytes 393224 | tf_op jit(solution)/shard_map/ppermute | solution.py:8
  12.2 1.4 %collective-permute-start.1 = (f32[256,128]{0,1:T(8,128)S(1)}, f32[256,128]{0,1:T(8,128)S(1)}, u32[]{:S(2)}, u32[]{:S(2)}) collective-permute-start(f32[256,128]{0,1:T(8,128)S(1)} %slice_bitcast_fusion.1), channel_id=1, source_target_pairs={{0,1},{1,0},{2,3},{3,2},{4,5},{5,4},{6,7},{7,6},{8,9},{9,8},{10,11... | collective-permute-start | bytes 393224 | tf_op jit(solution)/shard_map/ppermute | solution.py:8
  13.6 6.7 %collective-permute-start.2 = (f32[256,128]{0,1:T(8,128)S(1)}, f32[256,128]{0,1:T(8,128)S(1)}, u32[]{:S(2)}, u32[]{:S(2)}) collective-permute-start(f32[256,128]{0,1:T(8,128)S(1)} %fusion.117), channel_id=1, source_target_pairs={{0,2},{1,3},{2,0},{3,1},{4,6},{5,7},{6,4},{7,5},{8,10},{9,11},{10,... | collective-permute-start | bytes 393224 | tf_op jit(solution)/shard_map/ppermute | solution.py:8
  20.8 1.4 %collective-permute-start.3 = (f32[256,128]{0,1:T(8,128)S(1)}, f32[256,128]{0,1:T(8,128)S(1)}, u32[]{:S(2)}, u32[]{:S(2)}) collective-permute-start(f32[256,128]{0,1:T(8,128)S(1)} %slice_bitcast_fusion), channel_id=1, source_target_pairs={{0,1},{1,0},{2,3},{3,2},{4,5},{5,4},{6,7},{7,6},{8,9},{9,8},{10,11... | collective-permute-start | bytes 393224 | tf_op jit(solution)/shard_map/ppermute | solution.py:8
  22.3 5.6 %collective-permute-start.4 = (f32[256,128]{0,1:T(8,128)S(1)}, f32[256,128]{0,1:T(8,128)S(1)}, u32[]{:S(2)}, u32[]{:S(2)}) collective-permute-start(f32[256,128]{0,1:T(8,128)S(1)} %fusion.118), channel_id=1, source_target_pairs={{0,2},{1,3},{2,0},{3,1},{4,6},{5,7},{6,4},{7,5},{8,10},{9,11},{10,... | collective-permute-start | bytes 393224 | tf_op jit(solution)/shard_map/ppermute | solution.py:8
  27.9 5.0 %collective-permute-start.5 = (f32[256,128]{0,1:T(8,128)S(1)}, f32[256,128]{0,1:T(8,128)S(1)}, u32[]{:S(2)}, u32[]{:S(2)}) collective-permute-start(f32[256,128]{0,1:T(8,128)S(1)} %add.75), channel_id=1, source_target_pairs={{0,4},{1,5},{2,6},{3,7},{4,0},{5,1},{6,2},{7,3},{8,12},{9,13},{10,... | collective-permute-start | bytes 393224 | tf_op jit(solution)/shard_map/ppermute | solution.py:8
  33.3 1.4 %collective-permute-start.6 = (f32[256,128]{0,1:T(8,128)S(1)}, f32[256,128]{0,1:T(8,128)S(1)}, u32[]{:S(2)}, u32[]{:S(2)}) collective-permute-start(f32[256,128]{0,1:T(8,128)S(1)} %fusion.41), channel_id=1, source_target_pairs={{0,1},{1,0},{2,3},{3,2},{4,5},{5,4},{6,7},{7,6},{8,9},{9,8},{10,11... | collective-permute-start | bytes 393224 | tf_op jit(solution)/shard_map/ppermute | solution.py:8
  34.8 5.6 %collective-permute-start.7 = (f32[256,128]{0,1:T(8,128)S(1)}, f32[256,128]{0,1:T(8,128)S(1)}, u32[]{:S(2)}, u32[]{:S(2)}) collective-permute-start(f32[256,128]{0,1:T(8,128)S(1)} %add.78), channel_id=1, source_target_pairs={{0,2},{1,3},{2,0},{3,1},{4,6},{5,7},{6,4},{7,5},{8,10},{9,11},{10,... | collective-permute-start | bytes 393224 | tf_op jit(solution)/shard_map/ppermute | solution.py:8
  40.4 5.0 %collective-permute-start.8 = (f32[256,128]{0,1:T(8,128)S(1)}, f32[256,128]{0,1:T(8,128)S(1)}, u32[]{:S(2)}, u32[]{:S(2)}) collective-permute-start(f32[256,128]{0,1:T(8,128)S(1)} %add.79), channel_id=1, source_target_pairs={{0,4},{1,5},{2,6},{3,7},{4,0},{5,1},{6,2},{7,3},{8,12},{9,13},{10,... | collective-permute-start | bytes 393224 | tf_op jit(solution)/shard_map/ppermute | solution.py:8
  45.5 7.5 %collective-permute-start.9 = (f32[256,128]{0,1:T(8,128)S(1)}, f32[256,128]{0,1:T(8,128)S(1)}, u32[]{:S(2)}, u32[]{:S(2)}) collective-permute-start(f32[256,128]{0,1:T(8,128)S(1)} %add.80), channel_id=1, source_target_pairs={{0,8},{1,9},{2,10},{3,11},{4,12},{5,13},{6,14},{7,15},{8,0},{9,1},... | collective-permute-start | bytes 393224 | tf_op jit(solution)/shard_map/ppermute | solution.py:8
  53.3 1.4 %collective-permute-start.10 = (f32[256,128]{0,1:T(8,128)S(1)}, f32[256,128]{0,1:T(8,128)S(1)}, u32[]{:S(2)}, u32[]{:S(2)}) collective-permute-start(f32[256,128]{0,1:T(8,128)S(1)} %fusion.38), channel_id=1, source_target_pairs={{0,1},{1,0},{2,3},{3,2},{4,5},{5,4},{6,7},{7,6},{8,9},{9,8},{10,11... | collective-permute-start | bytes 393224 | tf_op jit(solution)/shard_map/ppermute | solution.py:8
  54.8 5.6 %collective-permute-start.11 = (f32[256,128]{0,1:T(8,128)S(1)}, f32[256,128]{0,1:T(8,128)S(1)}, u32[]{:S(2)}, u32[]{:S(2)}) collective-permute-start(f32[256,128]{0,1:T(8,128)S(1)} %add.82), channel_id=1, source_target_pairs={{0,2},{1,3},{2,0},{3,1},{4,6},{5,7},{6,4},{7,5},{8,10},{9,11},{10,... | collective-permute-start | bytes 393224 | tf_op jit(solution)/shard_map/ppermute | solution.py:8
  60.4 5.0 %collective-permute-start.12 = (f32[256,128]{0,1:T(8,128)S(1)}, f32[256,128]{0,1:T(8,128)S(1)}, u32[]{:S(2)}, u32[]{:S(2)}) collective-permute-start(f32[256,128]{0,1:T(8,128)S(1)} %add.83), channel_id=1, source_target_pairs={{0,4},{1,5},{2,6},{3,7},{4,0},{5,1},{6,2},{7,3},{8,12},{9,13},{10,... | collective-permute-start | bytes 393224 | tf_op jit(solution)/shard_map/ppermute | solution.py:8
  65.5 7.4 %collective-permute-start.13 = (f32[256,128]{0,1:T(8,128)S(1)}, f32[256,128]{0,1:T(8,128)S(1)}, u32[]{:S(2)}, u32[]{:S(2)}) collective-permute-start(f32[256,128]{0,1:T(8,128)S(1)} %add.84), channel_id=1, source_target_pairs={{0,8},{1,9},{2,10},{3,11},{4,12},{5,13},{6,14},{7,15},{8,0},{9,1},... | collective-permute-start | bytes 393224 | tf_op jit(solution)/shard_map/ppermute | solution.py:8
  73.1 1.4 %collective-permute-start.14 = (f32[256,128]{0,1:T(8,128)S(1)}, f32[256,128]{0,1:T(8,128)S(1)}, u32[]{:S(2)}, u32[]{:S(2)}) collective-permute-start(f32[256,128]{0,1:T(8,128)S(1)} %get-tuple-element.12), channel_id=1, source_target_pairs={{0,1},{1,0},{2,3},{3,2},{4,5},{5,4},{6,7},{7,6},{8,9},{9,8},{10,11... | collective-permute-start | bytes 393224 | tf_op jit(solution)/shard_map/ppermute | solution.py:8
  74.6 5.6 %collective-permute-start.15 = (f32[256,128]{0,1:T(8,128)S(1)}, f32[256,128]{0,1:T(8,128)S(1)}, u32[]{:S(2)}, u32[]{:S(2)}) collective-permute-start(f32[256,128]{0,1:T(8,128)S(1)} %add.86), channel_id=1, source_target_pairs={{0,2},{1,3},{2,0},{3,1},{4,6},{5,7},{6,4},{7,5},{8,10},{9,11},{10,... | collective-permute-start | bytes 393224 | tf_op jit(solution)/shard_map/ppermute | solution.py:8
  80.2 5.0 %collective-permute-start.16 = (f32[256,128]{0,1:T(8,128)S(1)}, f32[256,128]{0,1:T(8,128)S(1)}, u32[]{:S(2)}, u32[]{:S(2)}) collective-permute-start(f32[256,128]{0,1:T(8,128)S(1)} %add.87), channel_id=1, source_target_pairs={{0,4},{1,5},{2,6},{3,7},{4,0},{5,1},{6,2},{7,3},{8,12},{9,13},{10,... | collective-permute-start | bytes 393224 | tf_op jit(solution)/shard_map/ppermute | solution.py:8
  85.6 1.4 %collective-permute-start.17 = (f32[256,128]{0,1:T(8,128)S(1)}, f32[256,128]{0,1:T(8,128)S(1)}, u32[]{:S(2)}, u32[]{:S(2)}) collective-permute-start(f32[256,128]{0,1:T(8,128)S(1)} %get-tuple-element.14), channel_id=1, source_target_pairs={{0,1},{1,0},{2,3},{3,2},{4,5},{5,4},{6,7},{7,6},{8,9},{9,8},{10,11... | collective-permute-start | bytes 393224 | tf_op jit(solution)/shard_map/ppermute | solution.py:8
  87.0 5.6 %collective-permute-start.18 = (f32[256,128]{0,1:T(8,128)S(1)}, f32[256,128]{0,1:T(8,128)S(1)}, u32[]{:S(2)}, u32[]{:S(2)}) collective-permute-start(f32[256,128]{0,1:T(8,128)S(1)} %add.89), channel_id=1, source_target_pairs={{0,2},{1,3},{2,0},{3,1},{4,6},{5,7},{6,4},{7,5},{8,10},{9,11},{10,... | collective-permute-start | bytes 393224 | tf_op jit(solution)/shard_map/ppermute | solution.py:8
  93.0 1.4 %collective-permute-start.19 = (f32[256,128]{0,1:T(8,128)S(1)}, f32[256,128]{0,1:T(8,128)S(1)}, u32[]{:S(2)}, u32[]{:S(2)}) collective-permute-start(f32[256,128]{0,1:T(8,128)S(1)} %get-tuple-element.9), channel_id=1, source_target_pairs={{0,1},{1,0},{2,3},{3,2},{4,5},{5,4},{6,7},{7,6},{8,9},{9,8},{10,11... | collective-permute-start | bytes 393224 | tf_op jit(solution)/shard_map/ppermute | solution.py:8
where the time goes:
time: 101 us
  waiting for transfers between devices  56.8 us (56%)
  starting transfers between devices  22.6 us (22%)
  matrix products  14.8 us (15%)
  local copies, waits for them, and re-layouts  3.17 us (3%)
  other arithmetic  1.92 us (2%)
  between operations  1.57 us (2%)
    ppermute x20, waiting for transfers between devices, from_partner(): lax.ppermute(shard, axis, [(i, i ^ 1 << distance) for i in range(lax.axis...  56.8 us
    ppermute x20, starting transfers between devices, from_partner(): lax.ppermute(shard, axis, [(i, i ^ 1 << distance) for i in range(lax.axis...  22.6 us
    dot_general x1, matrix products, local(): jnp.einsum('vdu,vdo->vuo', leaf_diagonal_inverse, rounded_result(leaf_for...  4.95 us
    dot_general x1, matrix products, local(): jnp.einsum('ikab,ikbr->kar', leaf_coupling, masked, preferred_element_typ...  4.36 us
    unnamed x11, local copies, waits for them, and re-layouts  2.87 us
    dot_general x1, matrix products, local(): jnp.einsum('efj,ejs->efs', leaf_diagonal_inverse, rounded_result(leaf_rig...  2.86 us
  transfers between devices with their start and end apart: 20, of which 19 were waited for; matrix products, arithmetic and copies ran while one was open for 2% of the time, Pallas kernels for 0%

commit v1 on v0

v1 whole, which is shorter than its diff:
```python
import jax
import jax.numpy as jnp
from jax import lax
from jax.experimental import pallas as pl
from jax.experimental.pallas import tpu as pltpu
from jax.sharding import PartitionSpec as P

SMEM = pl.BlockSpec(memory_space=pltpu.SMEM)
VMEM = pl.BlockSpec(memory_space=pltpu.VMEM)
F32 = jnp.float32
BF16 = jnp.bfloat16


def swap(value, mask):
    count = lax.axis_size("col")
    return lax.ppermute(value, "col", [(i, i ^ mask) for i in range(count)])


def times(a, b):
    return lax.dot_general(a, b, (((1,), (0,)), ((), ())), preferred_element_type=F32)


def times_transposed(a, b):
    return lax.dot_general(a, b, (((1,), (1,)), ((), ())), preferred_element_type=F32)


def call(kernel, out_shape, in_specs, flops, bytes_accessed, name, **kwargs):
    return pl.pallas_call(
        kernel,
        out_shape=out_shape,
        in_specs=in_specs,
        name=name,
        cost_estimate=pl.CostEstimate(
            flops=flops, bytes_accessed=bytes_accessed, transcendentals=0
        ),
        **kwargs,
    )


def leaf_up(meta, pattern, right_hand, inverse, coupling, top_rhs):
    leaves, width, columns = right_hand.shape
    depth = coupling.shape[1]
    half = columns // 2

    def kernel(meta_ref, pat_ref, rhs_ref, inv_ref, cpl_ref, top_ref, fwd_ref, keep_ref, send_ref, acc):
        leaf = pl.program_id(0)
        solved = times(inv_ref[0], rhs_ref[0].astype(BF16))
        fwd_ref[0] = solved.T
        rounded = solved.astype(BF16)
        for k in range(depth):
            present = (pat_ref[leaf, k] != 0).astype(F32)
            term = present * times(cpl_ref[0, k], rounded)

            @pl.when(leaf == 0)
            def _():
                acc[k] = term

            @pl.when(leaf > 0)
            def _():
                acc[k] = acc[k] + term

        @pl.when(leaf == leaves - 1)
        def _():
            core = meta_ref[0]
            for k in range(depth):
                mine = (meta_ref[1] == k).astype(F32)
                acc[k] = acc[k] - mine * top_ref[0]
                flipped = acc[k].T

                @pl.when(core == 0)
                def _():
                    keep_ref[k] = flipped[:half]
                    send_ref[k] = flipped[half:]

                @pl.when(core != 0)
                def _():
                    keep_ref[k] = flipped[half:]
                    send_ref[k] = flipped[:half]

    part = jax.ShapeDtypeStruct((depth, half, width), F32)
    whole = pl.BlockSpec((depth, half, width), lambda i: (0, 0, 0))
    return call(
        kernel,
        (jax.ShapeDtypeStruct((leaves, columns, width), F32), part, part),
        [
            SMEM,
            SMEM,
            pl.BlockSpec((1, width, columns), lambda i: (i, 0, 0)),
            pl.BlockSpec((1, width, width), lambda i: (i, 0, 0)),
            pl.BlockSpec((1, depth, width, width), lambda i: (i, 0, 0, 0)),
            pl.BlockSpec((1, width, columns), lambda i: (0, 0, 0)),
        ],
        2 * leaves * (depth + 1) * width * width * columns,
        leaves * width * (width * 2 * (depth + 1) + columns * 8),
        "leaf_up",
        grid=(leaves,),
        out_specs=(pl.BlockSpec((1, columns, width), lambda i: (i, 0, 0)), whole, whole),
        scratch_shapes=[pltpu.VMEM((depth, width, columns), F32)],
    )(meta, pattern, right_hand, inverse, coupling, top_rhs)


def node_up(mine, theirs, factors, level, name):
    half, width = mine.shape

    def kernel(mine_ref, theirs_ref, w_ref, fwd_ref, *up_ref):
        total = mine_ref[...] + theirs_ref[...]
        solved = times_transposed((-total).astype(BF16), w_ref[0].astype(BF16))
        fwd_ref[...] = solved
        rounded = solved.astype(BF16)
        for k in range(level):
            up_ref[0][k] = times_transposed(rounded, w_ref[1 + k].astype(BF16))

    shapes = [jax.ShapeDtypeStruct((half, width), F32)]
    if level > 0:
        shapes.append(jax.ShapeDtypeStruct((level, half, width), F32))
    return call(
        kernel,
        tuple(shapes),
        [VMEM] * 3,
        2 * (1 + level) * half * width * width,
        4 * (1 + level) * width * width,
        name,
        out_specs=(VMEM,) * len(shapes),
    )(mine, theirs, factors)


def top_down(mine, theirs, forwards, factors):
    half, width = mine.shape
    levels = len(factors)
    n = len(forwards)

    def kernel(mine_ref, theirs_ref, *refs):
        fwd, w, out = refs[:n], refs[n : n + levels], refs[n + levels]
        total = mine_ref[...] + theirs_ref[...]
        inverse = w[0][0].astype(BF16)
        base = times_transposed((-total).astype(BF16), inverse)
        rounded = []
        for level in range(levels):
            if level > 0:
                base = fwd[level - 1][...]
                carried = times(rounded[0], w[level][1].astype(BF16))
                for k in range(1, level):
                    carried = carried + times(rounded[k], w[level][1 + k].astype(BF16))
                base = base - carried
            solved = times(base.astype(BF16), w[level][0].astype(BF16))
            out[level] = solved
            rounded.append(solved.astype(BF16))

    return call(
        kernel,
        jax.ShapeDtypeStruct((levels, half, width), F32),
        [VMEM] * (2 + n + levels),
        2 * (levels + 1) * half * width * width,
        4 * levels * width * width,
        "top_down",
        out_specs=VMEM,
    )(mine, theirs, *forwards, *factors)


def node_down(use_theirs, mine, theirs, forward, factors, name):
    level, half, width = mine.shape

    def kernel(flag_ref, mine_ref, theirs_ref, fwd_ref, w_ref, out_ref):
        take = flag_ref[0] != 0
        carried = None
        for k in range(level):
            known = jnp.where(take, theirs_ref[k], mine_ref[k])
            out_ref[k] = known
            term = times(known.astype(BF16), w_ref[1 + k].astype(BF16))
            carried = term if carried is None else carried + term
        base = (fwd_ref[...] - carried).astype(BF16)
        out_ref[level] = times(base, w_ref[0].astype(BF16))

    return call(
        kernel,
        jax.ShapeDtypeStruct((level + 1, half, width), F32),
        [SMEM] + [VMEM] * 4,
        2 * (1 + level) * half * width * width,
        4 * (1 + level) * width * width,
        name,
        out_specs=VMEM,
    )(use_theirs, mine, theirs, forward, factors)


def leaf_down(meta, pattern, mine, theirs, forward, inverse, coupling):
    leaves, columns, width = forward.shape
    depth = coupling.shape[1]
    half = columns // 2

    def kernel(meta_ref, pat_ref, mine_ref, theirs_ref, fwd_ref, inv_ref, cpl_ref, out_ref, top_ref, path):
        leaf = pl.program_id(0)

        @pl.when(leaf == 0)
        def _():
            core = meta_ref[0]
            own = jnp.maximum(meta_ref[1], 0)

            @pl.when(core == 0)
            def _():
                for k in range(depth):
                    path[k, :half] = mine_ref[k].astype(BF16)
                    path[k, half:] = theirs_ref[k].astype(BF16)
                top_ref[0, :, :] = jnp.concatenate([mine_ref[own], theirs_ref[own]], axis=0).T

            @pl.when(core != 0)
            def _():
                for k in range(depth):
                    path[k, :half] = theirs_ref[k].astype(BF16)
                    path[k, half:] = mine_ref[k].astype(BF16)
                top_ref[0, :, :] = jnp.concatenate([theirs_ref[own], mine_ref[own]], axis=0).T

        carried = jnp.zeros((columns, width), F32)
        for k in range(depth):
            present = (pat_ref[leaf, k] != 0).astype(F32)
            carried = carried + present * times(path[k], cpl_ref[0, k])
        base = (fwd_ref[0] - carried).astype(BF16)
        out_ref[0] = times(base, inv_ref[0]).T

    fixed = pl.BlockSpec((depth, half, width), lambda i: (0, 0, 0))
    return call(
        kernel,
        (
            jax.ShapeDtypeStruct((leaves, width, columns), F32),
            jax.ShapeDtypeStruct((1, width, columns), F32),
        ),
        [
            SMEM,
            SMEM,
            fixed,
            fixed,
            pl.BlockSpec((1, columns, width), lambda i: (i, 0, 0)),
            pl.BlockSpec((1, width, width), lambda i: (i, 0, 0)),
            pl.BlockSpec((1, depth, width, width), lambda i: (i, 0, 0, 0)),
        ],
        2 * leaves * (depth + 1) * width * width * columns,
        leaves * width * (width * 2 * (depth + 1) + columns * 8),
        "leaf_down",
        grid=(leaves,),
        out_specs=(
            pl.BlockSpec((1, width, columns), lambda i: (i, 0, 0)),
            pl.BlockSpec((1, width, columns), lambda i: (0, 0, 0)),
        ),
        scratch_shapes=[pltpu.VMEM((depth, columns, width), BF16)],
    )(meta, pattern, mine, theirs, forward, inverse, coupling)


def local(
    leaf_right_hand,
    leaf_diagonal_inverse,
    leaf_coupling,
    leaf_pattern,
    top_rhs,
    top_inverse,
    top_coupling,
):
    depth = lax.axis_size("col").bit_length() - 1
    device = lax.axis_index("col")
    width = top_inverse.shape[1]
    rows = width // 2

    def bit(b):
        return device >> b & 1

    core = bit(0)
    run, trailing = 1, 0
    for b in range(depth):
        run = run * bit(b)
        trailing = trailing + run
    own_level = depth - 1 - trailing
    meta = jnp.where(jnp.arange(2) == 0, core, own_level).astype(jnp.int32)

    own_factors = jnp.concatenate([top_inverse, top_coupling[0, : depth - 1]]).astype(F32)
    other_factors = swap(own_factors, 1)
    factors = [None] * depth
    factors[depth - 1] = jnp.where(core == 0, own_factors, other_factors)
    upper = jnp.where(core == 0, other_factors, own_factors)[: depth - 1]
    factors[depth - 2] = upper

    forward, keep, send = leaf_up(
        meta, leaf_pattern, leaf_right_hand, leaf_diagonal_inverse, leaf_coupling, top_rhs
    )

    def both_halves(part):
        other = swap(part, 1)
        first = jnp.where(core == 0, part, other)
        second = jnp.where(core == 0, other, part)
        return jnp.concatenate([first, second], axis=1)

    hub = swap(lax.dynamic_slice_in_dim(upper[: depth - 2], core * rows, rows, 1), 2)
    factors[depth - 3] = both_halves(hub)
    spread = [swap(hub[: depth - 3], 4 | m << 3) for m in range(1 << (depth - 3))]
    for b in range(3, depth):
        level = depth - 1 - b
        index = bit(b) << (b - 3)
        for i in range(3, b):
            index = index | (1 - bit(i)) << (i - 3)
        part = spread[0][: level + 1]
        for m in range(1, 1 << (b - 2)):
            part = jnp.where(index == m, spread[m][: level + 1], part)
        factors[level] = both_halves(part)

    theirs = swap(send, 1)
    forwards = [None] * depth
    rest = keep + theirs
    mine, other = keep[depth - 1], theirs[depth - 1]
    for level in reversed(range(1, depth)):
        solved, terms = node_up(mine, other, factors[level], level, f"node_up_{level}")
        forwards[level] = solved
        rest = rest[:level] + terms
        mine = rest[level - 1]
        other = swap(mine, 1 << (depth - level))
        if level > 1:
            rest = rest[: level - 1] + swap(rest[: level - 1], 1 << (depth - level))

    known = top_down(mine, other, forwards[1 : depth - 2], factors[: depth - 2])
    for level in (depth - 2, depth - 1):
        b = depth - level
        use_theirs = jnp.full((1,), bit(b), jnp.int32)
        known = node_down(
            use_theirs,
            known,
            swap(known, 1 << b),
            forwards[level],
            factors[level],
            f"node_down_{level}",
        )
    return leaf_down(
        meta,
        leaf_pattern,
        known,
        swap(known, 1),
        forward,
        leaf_diagonal_inverse,
        leaf_coupling,
    )


def solution(mesh):
    in_specs = (
        P(("grp", "col"), None, None),
        P(("grp", "col"), None, None),
        P(("grp", "col"), None, None, None),
        P(("grp", "col"), None),
        P(("grp", "col"), None, None),
        P(("grp", "col"), None, None),
        P(("grp", "col"), None, None, None),
    )
    out_specs = (P(("grp", "col"), None, None), P(("grp", "col"), None, None))
    return jax.shard_map(local, mesh=mesh, in_specs=in_specs, out_specs=out_specs, check_vma=False)
```

time: 101 us -> 97.3 us (0.963)
  Pallas kernels: 0 us -> 37.2 us
  waiting for transfers between devices: 56.8 us -> 26.9 us
  matrix products: 14.8 us -> 0 us
  starting transfers between devices: 22.6 us -> 15.7 us
  local copies, waits for them, and re-layouts: 3.17 us -> 8.79 us
  other arithmetic: 1.92 us -> 7.08 us
    pallas_call x0 -> x8, Pallas kernels: none -> 37.2 us  [the longest x1 13.4 us: leaf_up(): call(kernel, (jax.ShapeDtypeStruct((leaves, columns, width), F32), part,...]
    ppermute x20 -> x15, waiting for transfers between devices: 56.8 us -> 26.9 us  [swap(): return lax.ppermute(value, 'col', [(i, i ^ mask) for i in range(count)])]
    dot_general x14 -> x0, matrix products: 14.8 us -> none  [the longest x1 4.95 us: local(): jnp.einsum('vdu,vdo->vuo', leaf_diagonal_inverse, rounded_result(leaf_for...]
    ppermute x20 -> x15, starting transfers between devices: 22.6 us -> 15.7 us  [swap(): return lax.ppermute(value, 'col', [(i, i ^ mask) for i in range(count)])]
    squeeze x3 -> x4, local copies, waits for them, and re-layouts: 0.03 us -> 3.14 us  [the longest x2 2.11 us: local(): mine, other = (keep[depth - 1], theirs[depth - 1])]
    select_n x0 -> x5, other arithmetic: none -> 1.81 us  [the longest x1 1.17 us: local(): upper = jnp.where(core == 0, other_factors, own_factors)[:depth - 1]]
    unnamed x11 -> x25, local copies, waits for them, and re-layouts: 2.87 us -> 4.62 us
    add x12 -> x2, other arithmetic: 0.21 us -> 1.89 us  [local(): rest = rest[:level] + terms]
  transfers between devices with their start and end apart: 20 -> 15, of which waited for: 19 -> 8; matrix products, arithmetic and copies ran while one was open for 2% -> 8% of each run, Pallas kernels for 0% -> 21%
where the time goes in v1:
time: 97.3 us; the launch traced here: 96.4 us
  Pallas kernels  37.2 us (38%)
  waiting for transfers between devices  26.9 us (28%)
  starting transfers between devices  15.7 us (16%)
  local copies, waits for them, and re-layouts  8.79 us (9%)
  other arithmetic  7.08 us (7%)
    ppermute x15, waiting for transfers between devices, swap(): return lax.ppermute(value, 'col', [(i, i ^ mask) for i in range(count)])  26.9 us
    ppermute x15, starting transfers between devices, swap(): return lax.ppermute(value, 'col', [(i, i ^ mask) for i in range(count)])  15.7 us
    pallas_call x1, Pallas kernels, leaf_up(): call(kernel, (jax.ShapeDtypeStruct((leaves, columns, width), F32), part,...  13.4 us
    pallas_call x1, Pallas kernels, leaf_down(): call(kernel, (jax.ShapeDtypeStruct((leaves, width, columns), F32), jax.Sh...  9.89 us
    pallas_call x3, Pallas kernels, node_up(): call(kernel, tuple(shapes), [VMEM] * 3, 2 * (1 + level) * half * width *...  6.69 us
    pallas_call x2, Pallas kernels, node_down(): call(kernel, jax.ShapeDtypeStruct((level + 1, half, width), F32), [SMEM]...  4.8 us
    unnamed x25, local copies, waits for them, and re-layouts  4.62 us
    pallas_call x1, Pallas kernels, top_down(): call(kernel, jax.ShapeDtypeStruct((levels, half, width), F32), [VMEM] * (...  2.42 us
  transfers between devices with their start and end apart: 15, of which 8 were waited for; matrix products, arithmetic and copies ran while one was open for 8% of the time, Pallas kernels for 21%

profile of v1, /device:TPU:0, one launch (start us, length us, event | category | flops | bytes accessed | tf_op | source)
XLA Modules:
  0.0 96.4 jit_solution(17262147159965814025)
XLA Ops:
  0.6 0.0 copy-start.11
  0.6 1.0 %slice_bitcast_fusion = bf16[3,256,256]{2,1,0:T(8,128)(2,1)S(1)} fusion(bf16[1,4,256,256]{3,2,1,0:T(8,128)(2,1)} %param.13), kind=kLoop, calls=%fused_computation.4 | loop fusion | bytes 786432 | tf_op jit(solution)/shard_map/squeeze | solution.py:272
  1.7 1.0 %maximum_convert_fusion = f32[4,256,256]{2,1,0:T(8,128)S(1)} fusion(bf16[3,256,256]{2,1,0:T(8,128)(2,1)S(1)} %slice_bitcast_fusion, bf16[1,256,256]{2,1,0:T(8,128)(2,1)} %param.12), kind=kLoop, calls=%fused_computation | loop fusion | flops 524288 | bytes 1572864 | tf_op jit(solution)/shard_map/convert_element_type | solution.py:272
  2.7 0.6 collective-permute-start.1
  3.2 0.0 copy-done.11
  3.2 0.7 copy.10.pat_ref
  3.9 0.6 compare_select_fusion.meta_ref
  4.5 13.4 %leaf_up.1 = (f32[10,128,256]{2,1,0:T(8,128)}, f32[4,64,256]{2,1,0:T(8,128)}, f32[4,64,256]{2,1,0:T(8,128)}) custom-call(s32[2]{0:T(128)} %compare_select_fusion.meta_ref, s32[10,4]{1,0:T(8,128)} %copy.10.pat_ref, f32[10,256,128]{2,1,0:T(8,128)} %rhs_ref.1, bf16[10,256,256]{2,1,0:T(8,128)(2,1)} %inv_ref.3, bf16[10,4,256,256]{3,2,1,0:T(8,128)(2,1)} %cpl_ref.3, ...), custom_call_target="tpu_custom_call" | custom-call | flops 838860800 | bytes 9175040 | tf_op jit(solution)/shard_map/leaf_up/pallas_call | solution.py:82
  17.9 0.1 collective-permute-start
  18.0 1.5 %slice_bitcast_fusion.4.mine_ref = f32[64,256]{1,0:T(8,128)} fusion(f32[4,64,256]{2,1,0:T(8,128)} %get-tuple-element.11), kind=kLoop, calls=%fused_computation.15 | loop fusion | bytes 131072 | tf_op jit(solution)/shard_map/squeeze | solution.py:305
  19.5 0.2 collective-permute-done
  19.7 0.6 slice_bitcast_fusion.3.theirs_ref
  20.3 0.0 collective-permute-done.1
  20.3 0.0 copy-done
  20.3 1.2 %broadcast_select_fusion = (f32[4,256,256]{2,1,0:T(8,128)S(1)}, f32[4,256,256]{2,1,0:T(8,128)}) fusion(f32[4,256,256]{2,1,0:T(8,128)S(1)} %collective-permute-done.1, pred[]{:T(512)S(6)} %eq.7, bf16[3,256,256]{2,1,0:T(8,128)(2,1)S(1)} %slice_bitcast_fusion, bf16[1,256,256]{2,1,0:T(8,128)(2,1)S(1)} %copy-done), kind=kLoop, calls=%fused_computation.2 | loop fusion | flops 1048576 | bytes 3670017 | tf_op jit(solution)/shard_map/jit(_where)/select_n | solution.py:276
  21.6 2.8 %collective-permute-start.6 = (f32[2,128,256]{2,1,0:T(8,128)S(1)}, f32[2,128,256]{2,1,0:T(8,128)S(1)}, u32[]{:S(2)}, u32[]{:S(2)}) collective-permute-start(f32[2,128,256]{2,1,0:T(8,128)S(1)} %constant_dynamic-slice_fusion), channel_id=1, source_target_pairs={{0,2},{1,3},{2,0},{3,1},{4,6},{5,7},{6,4},{7,5},{8,10},{9,11},{10,... | collective-permute-start | bytes 786440 | tf_op jit(solution)/shard_map/ppermute | solution.py:16
  24.4 2.4 %node_up_3.1 = (f32[64,256]{1,0:T(8,128)}, f32[3,64,256]{2,1,0:T(8,128)}) custom-call(f32[64,256]{1,0:T(8,128)} %slice_bitcast_fusion.4.mine_ref, f32[64,256]{1,0:T(8,128)} %slice_bitcast_fusion.3.theirs_ref, f32[4,256,256]{2,1,0:T(8,128)} %get-tuple-element.21.w_ref), custom_call_target="tpu_custom_call" | custom-call | flops 33554432 | bytes 1048576 | tf_op jit(solution)/shard_map/node_up_3/pallas_call | solution.py:116
  26.8 0.0 copy-done.5
  26.8 1.0 fusion
  27.8 0.1 collective-permute-start.2
  27.9 0.0 copy-start.1
  27.9 2.1 %collective-permute-start.3 = (f32[64,256]{1,0:T(8,128)S(1)}, f32[64,256]{1,0:T(8,128)S(1)}, u32[]{:S(2)}, u32[]{:S(2)}) collective-permute-start(f32[64,256]{1,0:T(8,128)S(1)} %slice_bitcast_fusion.2.mine_ref), channel_id=1, source_target_pairs={{0,2},{1,3},{2,0},{3,1},{4,6},{5,7},{6,4},{7,5},{8,10},{9,11},{10,... | collective-permute-start | bytes 196616 | tf_op jit(solution)/shard_map/ppermute | solution.py:16
  29.9 0.9 slice.53.w_ref
  30.9 4.5 %collective-permute-done.3.theirs_ref = f32[64,256]{1,0:T(8,128)S(1)} collective-permute-done((f32[64,256]{1,0:T(8,128)S(1)}, f32[64,256]{1,0:T(8,128)S(1)}, u32[]{:S(2)}, u32[]{:S(2)}) %collective-permute-start.3) | collective-permute-done | bytes 65568 | tf_op jit(solution)/shard_map/ppermute | solution.py:16
  35.4 0.0 copy-done.1
  35.4 0.6 copy-done.8
  36.0 2.2 %node_up_2.1 = (f32[64,256]{1,0:T(8,128)}, f32[2,64,256]{2,1,0:T(8,128)}) custom-call(f32[64,256]{1,0:T(8,128)} %copy-done.1, f32[64,256]{1,0:T(8,128)} %copy-done.8, f32[3,256,256]{2,1,0:T(8,128)} %slice.53.w_ref), custom_call_target="tpu_custom_call" | custom-call | flops 25165824 | bytes 786432 | tf_op jit(solution)/shard_map/node_up_2/pallas_call | solution.py:116
  38.2 0.0 collective-permute-done.6
  38.3 1.9 %collective-permute-start.10 = (f32[1,128,256]{2,1,0:T(8,128)S(1)}, f32[1,128,256]{2,1,0:T(8,128)S(1)}, u32[]{:S(2)}, u32[]{:S(2)}) collective-permute-start(f32[1,128,256]{2,1,0:T(8,128)S(1)} %slice.57), channel_id=1, source_target_pairs={{0,4},{1,5},{2,6},{3,7},{4,0},{5,1},{6,2},{7,3},{8,12},{9,13},{10,... | collective-permute-start | bytes 393224 | tf_op jit(solution)/shard_map/ppermute | solution.py:16
  40.1 2.5 %collective-permute-start.9 = (f32[1,128,256]{2,1,0:T(8,128)S(1)}, f32[1,128,256]{2,1,0:T(8,128)S(1)}, u32[]{:S(2)}, u32[]{:S(2)}) collective-permute-start(f32[1,128,256]{2,1,0:T(8,128)S(1)} %slice.57), channel_id=1, source_target_pairs={{0,12},{1,13},{2,14},{3,15},{4,8},{5,9},{6,10},{7,11},{8,4},{9,5},... | collective-permute-start | bytes 393224 | tf_op jit(solution)/shard_map/ppermute | solution.py:16
  42.6 0.0 collective-permute-done.2
  42.6 0.9 add_add_fusion
  43.5 0.1 collective-permute-start.7
  43.6 0.0 collective-permute-done.10
  43.6 4.6 %collective-permute-done.9 = f32[1,128,256]{2,1,0:T(8,128)S(1)} collective-permute-done((f32[1,128,256]{2,1,0:T(8,128)S(1)}, f32[1,128,256]{2,1,0:T(8,128)S(1)}, u32[]{:S(2)}, u32[]{:S(2)}) %collective-permute-start.9) | collective-permute-done | bytes 131104 | tf_op jit(solution)/shard_map/ppermute | solution.py:16
  48.2 0.1 collective-permute-start.11
  48.3 0.0 copy-start.3
  48.3 0.7 collective-permute-start.4
  49.1 1.3 %collective-permute-start.5 = (f32[64,256]{1,0:T(8,128)S(1)}, f32[64,256]{1,0:T(8,128)S(1)}, u32[]{:S(2)}, u32[]{:S(2)}) collective-permute-start(f32[64,256]{1,0:T(8,128)S(1)} %get-tuple-element.27.mine_ref), channel_id=1, source_target_pairs={{0,4},{1,5},{2,6},{3,7},{4,0},{5,1},{6,2},{7,3},{8,12},{9,13},{10,... | collective-permute-start | bytes 196616 | tf_op jit(solution)/shard_map/ppermute | solution.py:16
  50.4 0.0 collective-permute-done.11
  50.4 0.0 collective-permute-done.7
  50.5 0.8 pad_maximum_fusion.w_ref.refs_2_
  51.3 2.9 %collective-permute-done.5.theirs_ref = f32[64,256]{1,0:T(8,128)S(1)} collective-permute-done((f32[64,256]{1,0:T(8,128)S(1)}, f32[64,256]{1,0:T(8,128)S(1)}, u32[]{:S(2)}, u32[]{:S(2)}) %collective-permute-start.5) | collective-permute-done | bytes 65568 | tf_op jit(solution)/shard_map/ppermute | solution.py:16
  54.3 0.6 copy-done.9
  54.9 2.1 %node_up_1.1 = (f32[64,256]{1,0:T(8,128)}, f32[1,64,256]{2,1,0:T(8,128)}) custom-call(f32[64,256]{1,0:T(8,128)} %copy-done.3, f32[64,256]{1,0:T(8,128)} %copy-done.9, f32[2,256,256]{2,1,0:T(8,128)} %pad_maximum_fusion.w_ref.refs_2_), custom_call_target="tpu_custom_call" | custom-call | flops 16777216 | bytes 524288 | tf_op jit(solution)/shard_map/node_up_1/pallas_call | solution.py:116
  57.0 0.0 collective-permute-done.4
  57.0 0.9 add_bitcast_fusion.mine_ref
  57.8 1.9 %collective-permute-start.8 = (f32[64,256]{1,0:T(8,128)S(1)}, f32[64,256]{1,0:T(8,128)S(1)}, u32[]{:S(2)}, u32[]{:S(2)}) collective-permute-start(f32[64,256]{1,0:T(8,128)S(1)} %add_bitcast_fusion.mine_ref), channel_id=1, source_target_pairs={{0,8},{1,9},{2,10},{3,11},{4,12},{5,13},{6,14},{7,15},{8,0},{9,1},... | collective-permute-start | bytes 196616 | tf_op jit(solution)/shard_map/ppermute | solution.py:16
  59.8 0.7 pad_maximum_fusion.1.refs_1_
  60.5 3.4 %collective-permute-done.8.theirs_ref = f32[64,256]{1,0:T(8,128)S(1)} collective-permute-done((f32[64,256]{1,0:T(8,128)S(1)}, f32[64,256]{1,0:T(8,128)S(1)}, u32[]{:S(2)}, u32[]{:S(2)}) %collective-permute-start.8) | collective-permute-done | bytes 65568 | tf_op jit(solution)/shard_map/ppermute | solution.py:16
  63.8 0.6 copy-done.10
  64.5 2.4 %top_down.1.mine_ref = f32[2,64,256]{2,1,0:T(8,128)} custom-call(f32[64,256]{1,0:T(8,128)} %copy-done.4, f32[64,256]{1,0:T(8,128)} %copy-done.10, f32[64,256]{1,0:T(8,128)} %get-tuple-element.16.refs_0_, f32[1,256,256]{2,1,0:T(8,128)} %pad_maximum_fusion.1.refs_1_, f32[2,256,256]{2,1,0:T(8,128)} %pad_maximum_fusion.w_ref.refs_2_), custom_call_target="tpu_custom_call" | custom-call | flops 25165824 | bytes 524288 | tf_op jit(solution)/shard_map/top_down/pallas_call | solution.py:149
  66.9 0.0 collective-permute-start.12
  66.9 5.2 %collective-permute-done.12.theirs_ref = f32[2,64,256]{2,1,0:T(8,128)S(1)} collective-permute-done((f32[2,64,256]{2,1,0:T(8,128)}, f32[2,64,256]{2,1,0:T(8,128)S(1)}, u32[]{:S(2)}, u32[]{:S(2)}) %collective-permute-start.12) | collective-permute-done | bytes 131104 | tf_op jit(solution)/shard_map/ppermute | solution.py:16
  72.1 0.6 copy-done.7
  72.7 2.3 %node_down_2.1.mine_ref = f32[3,64,256]{2,1,0:T(8,128)} custom-call(s32[1]{0:T(128)} %bitcast.1.flag_ref, f32[2,64,256]{2,1,0:T(8,128)} %top_down.1.mine_ref, f32[2,64,256]{2,1,0:T(8,128)} %copy-done.7, f32[64,256]{1,0:T(8,128)} %get-tuple-element.17.fwd_ref, f32[3,256,256]{2,1,0:T(8,128)} %slice.53.w_ref), custom_call_target="tpu_custom_call" | custom-call | flops 25165824 | bytes 786432 | tf_op jit(solution)/shard_map/node_down_2/pallas_call | solution.py:174
  75.0 1.5 %collective-permute-start.13 = (f32[3,64,256]{2,1,0:T(8,128)}, f32[3,64,256]{2,1,0:T(8,128)S(1)}, u32[]{:S(2)}, u32[]{:S(2)}) collective-permute-start(f32[3,64,256]{2,1,0:T(8,128)} %node_down_2.1.mine_ref), channel_id=1, source_target_pairs={{0,2},{1,3},{2,0},{3,1},{4,6},{5,7},{6,4},{7,5},{8,10},{9,11},{10,... | collective-permute-start | bytes 589832 | tf_op jit(solution)/shard_map/ppermute | solution.py:16
  76.5 4.4 %collective-permute-done.13.theirs_ref = f32[3,64,256]{2,1,0:T(8,128)S(1)} collective-permute-done((f32[3,64,256]{2,1,0:T(8,128)}, f32[3,64,256]{2,1,0:T(8,128)S(1)}, u32[]{:S(2)}, u32[]{:S(2)}) %collective-permute-start.13) | collective-permute-done | bytes 196640 | tf_op jit(solution)/shard_map/ppermute | solution.py:16
  80.9 0.7 copy-done.6
  81.6 2.5 %node_down_3.1.mine_ref = f32[4,64,256]{2,1,0:T(8,128)} custom-call(s32[1]{0:T(128)} %bitcast.flag_ref, f32[3,64,256]{2,1,0:T(8,128)} %node_down_2.1.mine_ref, f32[3,64,256]{2,1,0:T(8,128)} %copy-done.6, f32[64,256]{1,0:T(8,128)} %get-tuple-element.18.fwd_ref, f32[4,256,256]{2,1,0:T(8,128)} %get-tuple-element.21.w_ref), custom_call_target="tpu_custom_call" | custom-call | flops 33554432 | bytes 1048576 | tf_op jit(solution)/shard_map/node_down_3/pallas_call | solution.py:174
  84.1 0.0 collective-permute-start.14
  84.1 1.7 %collective-permute-done.14.theirs_ref = f32[4,64,256]{2,1,0:T(8,128)S(1)} collective-permute-done((f32[4,64,256]{2,1,0:T(8,128)}, f32[4,64,256]{2,1,0:T(8,128)S(1)}, u32[]{:S(2)}, u32[]{:S(2)}) %collective-permute-start.14) | collective-permute-done | bytes 262176 | tf_op jit(solution)/shard_map/ppermute | solution.py:16
  85.8 0.7 copy-done.2
  86.5 9.9 %leaf_down.1 = (f32[10,256,128]{2,1,0:T(8,128)}, f32[1,256,128]{2,1,0:T(8,128)}) custom-call(s32[2]{0:T(128)} %compare_select_fusion.meta_ref, s32[10,4]{1,0:T(8,128)} %copy.10.pat_ref, f32[4,64,256]{2,1,0:T(8,128)} %node_down_3.1.mine_ref, f32[4,64,256]{2,1,0:T(8,128)} %copy-done.2, f32[10,128,256]{2,1,0:T(8,128)} %get-tuple-element.19.fwd_ref, ...), custom_call_target="tpu_custom_call" | custom-call | flops 838860800 | bytes 9175040 | tf_op jit(solution)/shard_map/leaf_down/pallas_call | solution.py:220
  (20 shorter events, 0.2 us)
Async XLA Ops:
  0.6 2.6 %copy-start.11 = (s32[10,4]{0,1:T(4,128)S(1)}, s32[10,4]{0,1:T(4,128)}, u32[]{:S(2)}) copy-start(s32[10,4]{0,1:T(4,128)} %param.10) | copy-start | bytes 484
  2.7 17.7 %collective-permute-start.1 = (f32[4,256,256]{2,1,0:T(8,128)S(1)}, f32[4,256,256]{2,1,0:T(8,128)S(1)}, u32[]{:S(2)}, u32[]{:S(2)}) collective-permute-start(f32[4,256,256]{2,1,0:T(8,128)S(1)} %maximum_convert_fusion), channel_id=1, source_target_pairs={{0,1},{1,0},{2,3},{3,2},{4,5},{5,4},{6,7},{7,6},{8,9},{9,8},{10,11... | collective-permute-start | bytes 3145736 | tf_op jit(solution)/shard_map/ppermute | solution.py:16
  4.5 15.9 %copy-start = (bf16[1,256,256]{2,1,0:T(8,128)(2,1)S(1)}, bf16[1,256,256]{2,1,0:T(8,128)(2,1)}, u32[]{:S(2)}) copy-start(bf16[1,256,256]{2,1,0:T(8,128)(2,1)} %param.12) | copy-start | bytes 393220
  17.9 1.8 %collective-permute-start = (f32[4,64,256]{2,1,0:T(8,128)}, f32[4,64,256]{2,1,0:T(8,128)S(1)}, u32[]{:S(2)}, u32[]{:S(2)}) collective-permute-start(f32[4,64,256]{2,1,0:T(8,128)} %get-tuple-element.12), channel_id=1, source_target_pairs={{0,1},{1,0},{2,3},{3,2},{4,5},{5,4},{6,7},{7,6},{8,9},{9,8},{10,11... | collective-permute-start | bytes 786440 | tf_op jit(solution)/shard_map/ppermute | solution.py:16
  21.5 5.3 %copy-start.5 = (f32[4,64,256]{2,1,0:T(8,128)S(1)}, f32[4,64,256]{2,1,0:T(8,128)}, u32[]{:S(2)}) copy-start(f32[4,64,256]{2,1,0:T(8,128)} %get-tuple-element.11) | copy-start | bytes 786436
  21.6 16.7 %collective-permute-start.6 = (f32[2,128,256]{2,1,0:T(8,128)S(1)}, f32[2,128,256]{2,1,0:T(8,128)S(1)}, u32[]{:S(2)}, u32[]{:S(2)}) collective-permute-start(f32[2,128,256]{2,1,0:T(8,128)S(1)} %constant_dynamic-slice_fusion), channel_id=1, source_target_pairs={{0,2},{1,3},{2,0},{3,1},{4,6},{5,7},{6,4},{7,5},{8,10},{9,11},{10,... | collective-permute-start | bytes 786440 | tf_op jit(solution)/shard_map/ppermute | solution.py:16
  27.8 14.8 %collective-permute-start.2 = (f32[2,64,256]{2,1,0:T(8,128)S(1)}, f32[2,64,256]{2,1,0:T(8,128)S(1)}, u32[]{:S(2)}, u32[]{:S(2)}) collective-permute-start(f32[2,64,256]{2,1,0:T(8,128)S(1)} %slice.51), channel_id=1, source_target_pairs={{0,2},{1,3},{2,0},{3,1},{4,6},{5,7},{6,4},{7,5},{8,10},{9,11},{10,... | collective-permute-start | bytes 393224 | tf_op jit(solution)/shard_map/ppermute | solution.py:16
  27.9 7.5 %copy-start.1 = (f32[64,256]{1,0:T(8,128)}, f32[64,256]{1,0:T(8,128)S(1)}, u32[]{:S(2)}) copy-start(f32[64,256]{1,0:T(8,128)S(1)} %slice_bitcast_fusion.2.mine_ref) | copy-start | bytes 196612
  27.9 7.5 %collective-permute-start.3 = (f32[64,256]{1,0:T(8,128)S(1)}, f32[64,256]{1,0:T(8,128)S(1)}, u32[]{:S(2)}, u32[]{:S(2)}) collective-permute-start(f32[64,256]{1,0:T(8,128)S(1)} %slice_bitcast_fusion.2.mine_ref), channel_id=1, source_target_pairs={{0,2},{1,3},{2,0},{3,1},{4,6},{5,7},{6,4},{7,5},{8,10},{9,11},{10,... | collective-permute-start | bytes 196616 | tf_op jit(solution)/shard_map/ppermute | solution.py:16
  35.4 0.6 copy-start.8
  38.3 5.4 %collective-permute-start.10 = (f32[1,128,256]{2,1,0:T(8,128)S(1)}, f32[1,128,256]{2,1,0:T(8,128)S(1)}, u32[]{:S(2)}, u32[]{:S(2)}) collective-permute-start(f32[1,128,256]{2,1,0:T(8,128)S(1)} %slice.57), channel_id=1, source_target_pairs={{0,4},{1,5},{2,6},{3,7},{4,0},{5,1},{6,2},{7,3},{8,12},{9,13},{10,... | collective-permute-start | bytes 393224 | tf_op jit(solution)/shard_map/ppermute | solution.py:16
  40.1 8.1 %collective-permute-start.9 = (f32[1,128,256]{2,1,0:T(8,128)S(1)}, f32[1,128,256]{2,1,0:T(8,128)S(1)}, u32[]{:S(2)}, u32[]{:S(2)}) collective-permute-start(f32[1,128,256]{2,1,0:T(8,128)S(1)} %slice.57), channel_id=1, source_target_pairs={{0,12},{1,13},{2,14},{3,15},{4,8},{5,9},{6,10},{7,11},{8,4},{9,5},... | collective-permute-start | bytes 393224 | tf_op jit(solution)/shard_map/ppermute | solution.py:16
  43.5 6.9 %collective-permute-start.7 = (f32[2,128,256]{2,1,0:T(8,128)S(1)}, f32[2,128,256]{2,1,0:T(8,128)S(1)}, u32[]{:S(2)}, u32[]{:S(2)}) collective-permute-start(f32[2,128,256]{2,1,0:T(8,128)S(1)} %collective-permute-done.6), channel_id=1, source_target_pairs={{0,1},{1,0},{2,3},{3,2},{4,5},{5,4},{6,7},{7,6},{8,9},{9,8},{10,11... | collective-permute-start | bytes 786440 | tf_op jit(solution)/shard_map/ppermute | solution.py:16
  48.2 2.2 %collective-permute-start.11 = (f32[1,128,256]{2,1,0:T(8,128)S(1)}, f32[1,128,256]{2,1,0:T(8,128)S(1)}, u32[]{:S(2)}, u32[]{:S(2)}) collective-permute-start(f32[1,128,256]{2,1,0:T(8,128)S(1)} %broadcast_select_fusion.4), channel_id=1, source_target_pairs={{0,1},{1,0},{2,3},{3,2},{4,5},{5,4},{6,7},{7,6},{8,9},{9,8},{10,11... | collective-permute-start | bytes 393224 | tf_op jit(solution)/shard_map/ppermute | solution.py:16
  48.3 3.0 %copy-start.3 = (f32[64,256]{1,0:T(8,128)}, f32[64,256]{1,0:T(8,128)S(1)}, u32[]{:S(2)}) copy-start(f32[64,256]{1,0:T(8,128)S(1)} %get-tuple-element.27.mine_ref) | copy-start | bytes 196612
  48.3 8.6 %collective-permute-start.4 = (f32[1,64,256]{2,1,0:T(8,128)S(1)}, f32[1,64,256]{2,1,0:T(8,128)S(1)}, u32[]{:S(2)}, u32[]{:S(2)}) collective-permute-start(f32[1,64,256]{2,1,0:T(8,128)S(1)} %get-tuple-element.26), channel_id=1, source_target_pairs={{0,4},{1,5},{2,6},{3,7},{4,0},{5,1},{6,2},{7,3},{8,12},{9,13},{10,... | collective-permute-start | bytes 196616 | tf_op jit(solution)/shard_map/ppermute | solution.py:16
  49.1 5.2 %collective-permute-start.5 = (f32[64,256]{1,0:T(8,128)S(1)}, f32[64,256]{1,0:T(8,128)S(1)}, u32[]{:S(2)}, u32[]{:S(2)}) collective-permute-start(f32[64,256]{1,0:T(8,128)S(1)} %get-tuple-element.27.mine_ref), channel_id=1, source_target_pairs={{0,4},{1,5},{2,6},{3,7},{4,0},{5,1},{6,2},{7,3},{8,12},{9,13},{10,... | collective-permute-start | bytes 196616 | tf_op jit(solution)/shard_map/ppermute | solution.py:16
  54.3 0.6 copy-start.9
  57.8 6.0 %copy-start.4 = (f32[64,256]{1,0:T(8,128)}, f32[64,256]{1,0:T(8,128)S(1)}, u32[]{:S(2)}) copy-start(f32[64,256]{1,0:T(8,128)S(1)} %add_bitcast_fusion.mine_ref) | copy-start | bytes 196612
  57.8 6.0 %collective-permute-start.8 = (f32[64,256]{1,0:T(8,128)S(1)}, f32[64,256]{1,0:T(8,128)S(1)}, u32[]{:S(2)}, u32[]{:S(2)}) collective-permute-start(f32[64,256]{1,0:T(8,128)S(1)} %add_bitcast_fusion.mine_ref), channel_id=1, source_target_pairs={{0,8},{1,9},{2,10},{3,11},{4,12},{5,13},{6,14},{7,15},{8,0},{9,1},... | collective-permute-start | bytes 196616 | tf_op jit(solution)/shard_map/ppermute | solution.py:16
  63.8 0.6 copy-start.10
  66.9 5.2 %collective-permute-start.12 = (f32[2,64,256]{2,1,0:T(8,128)}, f32[2,64,256]{2,1,0:T(8,128)S(1)}, u32[]{:S(2)}, u32[]{:S(2)}) collective-permute-start(f32[2,64,256]{2,1,0:T(8,128)} %top_down.1.mine_ref), channel_id=1, source_target_pairs={{0,4},{1,5},{2,6},{3,7},{4,0},{5,1},{6,2},{7,3},{8,12},{9,13},{10,... | collective-permute-start | bytes 393224 | tf_op jit(solution)/shard_map/ppermute | solution.py:16
  72.1 0.6 copy-start.7
  75.0 5.9 %collective-permute-start.13 = (f32[3,64,256]{2,1,0:T(8,128)}, f32[3,64,256]{2,1,0:T(8,128)S(1)}, u32[]{:S(2)}, u32[]{:S(2)}) collective-permute-start(f32[3,64,256]{2,1,0:T(8,128)} %node_down_2.1.mine_ref), channel_id=1, source_target_pairs={{0,2},{1,3},{2,0},{3,1},{4,6},{5,7},{6,4},{7,5},{8,10},{9,11},{10,... | collective-permute-start | bytes 589832 | tf_op jit(solution)/shard_map/ppermute | solution.py:16
  80.9 0.7 copy-start.6
  84.1 1.7 %collective-permute-start.14 = (f32[4,64,256]{2,1,0:T(8,128)}, f32[4,64,256]{2,1,0:T(8,128)S(1)}, u32[]{:S(2)}, u32[]{:S(2)}) collective-permute-start(f32[4,64,256]{2,1,0:T(8,128)} %node_down_3.1.mine_ref), channel_id=1, source_target_pairs={{0,1},{1,0},{2,3},{3,2},{4,5},{5,4},{6,7},{7,6},{8,9},{9,8},{10,11... | collective-permute-start | bytes 786440 | tf_op jit(solution)/shard_map/ppermute | solution.py:16
  85.8 0.7 copy-start.2

commit v2 on v0

v2 whole, which is shorter than its diff:
```python
import jax
import jax.numpy as jnp
from jax import lax
from jax.experimental import pallas as pl
from jax.experimental.pallas import tpu as pltpu
from jax.sharding import PartitionSpec as P

F32 = jnp.float32
BF16 = jnp.bfloat16
ANY = pl.BlockSpec(memory_space=pl.ANY)
VMEM = pl.BlockSpec(memory_space=pltpu.VMEM)


def swap(value, mask):
    count = lax.axis_size("col")
    return lax.ppermute(value, "col", [(i, i ^ mask) for i in range(count)])


def dot(a, b, dim_a, dim_b):
    return lax.dot_general(a, b, (((dim_a,), (dim_b,)), ((), ())), preferred_element_type=F32)


def bit_of(b):
    return lax.axis_index("col") >> b & 1


def level_of_own_node():
    depth = lax.axis_size("col").bit_length() - 1
    run, trailing = 1, 0
    for b in range(depth):
        run = run * bit_of(b)
        trailing = trailing + run
    return depth - 1 - trailing


def call(kernel, name, outs, ins, flops=0, hbm_ins=(), hbm_outs=(), scratch=(), limit=4 << 20):
    pinned = [pltpu.with_memory_space_constraint(x, pltpu.VMEM) for x in ins]
    shapes = [jax.ShapeDtypeStruct(s, d) for s, d in hbm_outs] + [pltpu.VMEM(s, d) for s, d in outs]
    moved = sum(x.size * x.dtype.itemsize for x in hbm_ins)
    result = pl.pallas_call(
        kernel,
        out_shape=tuple(shapes),
        in_specs=[ANY] * len(hbm_ins) + [VMEM] * len(ins),
        out_specs=tuple([ANY] * len(hbm_outs) + [VMEM] * len(outs)),
        scratch_shapes=list(scratch),
        name=name,
        compiler_params=pltpu.CompilerParams(vmem_limit_bytes=limit),
        cost_estimate=pl.CostEstimate(flops=flops, bytes_accessed=moved + 1024, transcendentals=0),
    )(*hbm_ins, *pinned)
    return result


def split_columns(terms, keep_ref, send_ref, place):
    half = terms.shape[0] // 2

    @pl.when(bit_of(0) == 0)
    def _():
        keep_ref[place] = terms[:half]
        send_ref[place] = terms[half:]

    @pl.when(bit_of(0) != 0)
    def _():
        keep_ref[place] = terms[half:]
        send_ref[place] = terms[:half]


def leaf_terms(first, pattern, coupling, levels, top_rhs, right_hand=None, inverse=None, rounded=None):
    leaves, _, width, _ = coupling.shape
    columns = top_rhs.shape[2]
    half = columns // 2
    n = len(levels)
    start = levels[0]

    def kernel(pat_hbm, cpl_hbm, top_ref, *refs):
        if first:
            rhs_ref, inv_ref, keep_ref, send_ref, cpl_ref, fwd_ref, rnd_ref, pat_ref, pat_sem, sem = refs
        else:
            rnd_ref, keep_ref, send_ref, cpl_ref, pat_ref, pat_sem, sem = refs
        get_pattern = pltpu.make_async_copy(pat_hbm, pat_ref, pat_sem)
        get_pattern.start()
        fetches = []
        for i in range(leaves):
            fetch = pltpu.make_async_copy(cpl_hbm.at[i, pl.ds(start, n)], cpl_ref.at[i], sem.at[i])
            fetch.start()
            fetches.append(fetch)
        if first:
            for i in range(leaves):
                solved = dot(rhs_ref[i].astype(BF16), inv_ref[i], 0, 1)
                fwd_ref[i] = solved
                rnd_ref[i] = solved.astype(BF16)
        get_pattern.wait()
        sums = [None] * n
        for i in range(leaves):
            fetches[i].wait()
            for k in range(n):
                present = (pat_ref[start + k, i] != 0).astype(BF16)
                term = dot(rnd_ref[i] * present, cpl_ref[i, k], 1, 1)
                sums[k] = term if sums[k] is None else sums[k] + term
        own_rhs = top_ref[0].T
        for k in range(n):
            mine = (level_of_own_node() == start + k).astype(F32)
            split_columns(sums[k] - mine * own_rhs, keep_ref, send_ref, k)

    outs = [((n, half, width), F32)] * 2 + [((leaves, n, width, width), BF16)]
    ins = [top_rhs]
    if first:
        outs += [((leaves, columns, width), F32), ((leaves, columns, width), BF16)]
        ins += [right_hand, inverse]
    else:
        ins += [rounded]
    return call(
        kernel,
        "leaf_first" if first else "leaf_rest",
        outs,
        ins,
        2 * leaves * (n + first) * columns * width * width,
        hbm_ins=[pattern, coupling],
        scratch=[
            pltpu.SMEM(pattern.shape, jnp.int32),
            pltpu.SemaphoreType.DMA,
            pltpu.SemaphoreType.DMA((leaves,)),
        ],
    )


def own_factors(top_inverse, top_coupling):
    _, depth, width, _ = top_coupling.shape

    def kernel(inv_hbm, cpl_hbm, out_ref, raw, sem):
        a = pltpu.make_async_copy(inv_hbm.at[0], raw.at[0], sem.at[0])
        b = pltpu.make_async_copy(cpl_hbm.at[0, pl.ds(0, depth - 1)], raw.at[pl.ds(1, depth - 1)], sem.at[1])
        a.start()
        b.start()
        a.wait()
        b.wait()
        for k in range(depth):
            out_ref[k] = raw[k].astype(F32)

    return call(
        kernel,
        "own_factors",
        [((depth, width, width), F32)],
        [],
        hbm_ins=[top_inverse, top_coupling],
        scratch=[pltpu.VMEM((depth, width, width), BF16), pltpu.SemaphoreType.DMA((2,))],
    )[0]


def chip_factors(own, other):
    depth, width, _ = own.shape
    rows = width // 2

    def kernel(own_ref, other_ref, low_ref, high_ref, send_ref):
        def place(low, high, offset):
            for k in range(depth):
                low_ref[k] = low[k].astype(BF16)
            for k in range(depth - 1):
                high_ref[k] = high[k].astype(BF16)
            for k in range(depth - 2):
                send_ref[k] = high[k, offset : offset + rows]

        @pl.when(bit_of(0) == 0)
        def _():
            place(own_ref, other_ref, 0)

        @pl.when(bit_of(0) != 0)
        def _():
            place(other_ref, own_ref, rows)

    return call(
        kernel,
        "chip_factors",
        [((depth, width, width), BF16), ((depth - 1, width, width), BF16), ((depth - 2, rows, width), F32)],
        [own, other],
    )


def join_rows(mine, other, name):
    count, rows, width = mine.shape

    def kernel(mine_ref, other_ref, out_ref):
        @pl.when(bit_of(0) == 0)
        def _():
            out_ref[:, :rows] = mine_ref[...].astype(BF16)
            out_ref[:, rows:] = other_ref[...].astype(BF16)

        @pl.when(bit_of(0) != 0)
        def _():
            out_ref[:, rows:] = mine_ref[...].astype(BF16)
            out_ref[:, :rows] = other_ref[...].astype(BF16)

    return call(kernel, name, [((count, 2 * rows, width), BF16)], [mine, other])[0]


def pick(parts, b, count, name):
    _, rows, width = parts[0].shape

    def kernel(*refs):
        index = bit_of(b) << (b - 3)
        for i in range(3, b):
            index = index | (1 - bit_of(i)) << (i - 3)
        for m in range(1 << (b - 2)):

            @pl.when(index == m)
            def _(m=m):
                refs[-1][...] = refs[m][:count]

    return call(kernel, name, [((count, rows, width), F32)], parts[: 1 << (b - 2)])[0]


def node_up(mine, theirs, factors, level):
    half, width = mine.shape[-2:]

    def kernel(mine_ref, theirs_ref, w_ref, fwd_ref, up_ref):
        total = mine_ref[0] + theirs_ref[0]
        solved = dot((-total).astype(BF16), w_ref[0], 1, 1)
        fwd_ref[...] = solved
        rounded = solved.astype(BF16)
        for k in range(level):
            up_ref[k] = dot(rounded, w_ref[1 + k], 1, 1)

    return call(
        kernel,
        f"node_up_{level}",
        [((half, width), F32), ((level, half, width), F32)],
        [mine, theirs, factors],
        2 * (1 + level) * half * width * width,
    )


def add_terms(up, mine, theirs):
    level, half, width = up.shape

    def kernel(up_ref, mine_ref, theirs_ref, next_ref, *rest_ref):
        for k in range(level):
            total = up_ref[k] + (mine_ref[k] + theirs_ref[k])
            if k == level - 1:
                next_ref[0] = total
            else:
                rest_ref[0][k] = total

    outs = [((1, half, width), F32)]
    if level > 1:
        outs.append(((level - 1, half, width), F32))
    return call(kernel, f"add_terms_{level}", outs, [up, mine, theirs])


def top_down(mine, theirs, forwards, factors):
    half, width = mine.shape[-2:]
    levels = len(factors)
    n = len(forwards)

    def kernel(mine_ref, theirs_ref, *refs):
        fwd, w, out = refs[:n], refs[n : n + levels], refs[n + levels]
        total = mine_ref[0] + theirs_ref[0]
        base = dot((-total).astype(BF16), w[0][0], 1, 1)
        rounded = []
        for level in range(levels):
            if level > 0:
                carried = dot(rounded[0], w[level][1], 1, 0)
                for k in range(1, level):
                    carried = carried + dot(rounded[k], w[level][1 + k], 1, 0)
                base = fwd[level - 1][...] - carried
            solved = dot(base.astype(BF16), w[level][0], 1, 0)
            out[level] = solved
            rounded.append(solved.astype(BF16))

    return call(
        kernel,
        "top_down",
        [((levels, half, width), F32)],
        [mine, theirs, *forwards, *factors],
        2 * (levels + 1) * half * width * width,
    )[0]


def node_down(b, mine, theirs, forward, factors):
    level, half, width = mine.shape

    def kernel(mine_ref, theirs_ref, fwd_ref, w_ref, out_ref):
        take = bit_of(b) != 0
        carried = None
        for k in range(level):
            known = jnp.where(take, theirs_ref[k], mine_ref[k])
            out_ref[k] = known
            term = dot(known.astype(BF16), w_ref[1 + k], 1, 0)
            carried = term if carried is None else carried + term
        base = (fwd_ref[...] - carried).astype(BF16)
        out_ref[level] = dot(base, w_ref[0], 1, 0)

    return call(
        kernel,
        f"node_down_{level}",
        [((level + 1, half, width), F32)],
        [mine, theirs, forward, factors],
        2 * (1 + level) * half * width * width,
    )[0]


def leaf_down(pattern, mine, theirs, forward, inverse, couplings):
    leaves, columns, width = forward.shape
    depth, half, _ = mine.shape
    n = len(couplings)
    where = [(g, k) for g in range(n) for k in range(couplings[g].shape[1])]

    def kernel(pat_hbm, *refs):
        mine_ref, theirs_ref, fwd_ref, inv_ref = refs[:4]
        cpl = refs[4 : 4 + n]
        out_hbm, top_hbm, out, top, path, pat_ref, pat_sem, sem = refs[4 + n :]
        get_pattern = pltpu.make_async_copy(pat_hbm, pat_ref, pat_sem)
        get_pattern.start()
        own = jnp.maximum(level_of_own_node(), 0)

        def gather(low, high):
            for k in range(depth):
                path[k, :half] = low[k].astype(BF16)
                path[k, half:] = high[k].astype(BF16)
            top[...] = jnp.concatenate([low[own], high[own]], axis=0).T

        @pl.when(bit_of(0) == 0)
        def _():
            gather(mine_ref, theirs_ref)

        @pl.when(bit_of(0) != 0)
        def _():
            gather(theirs_ref, mine_ref)

        put_top = pltpu.make_async_copy(top, top_hbm.at[0], sem.at[leaves])
        put_top.start()
        get_pattern.wait()
        puts = []
        for i in range(leaves):
            carried = None
            for level, (g, k) in enumerate(where):
                present = (pat_ref[level, i] != 0).astype(BF16)
                term = dot(path[level] * present, cpl[g][i, k], 1, 0)
                carried = term if carried is None else carried + term
            base = (fwd_ref[i] - carried).astype(BF16)
            out[i] = dot(base, inv_ref[i], 1, 0).T
            put = pltpu.make_async_copy(out.at[i], out_hbm.at[i], sem.at[i])
            put.start()
            puts.append(put)
        for put in puts:
            put.wait()
        put_top.wait()

    return call(
        kernel,
        "leaf_down",
        [],
        [mine, theirs, forward, inverse, *couplings],
        2 * leaves * (depth + 1) * columns * width * width,
        hbm_ins=[pattern],
        hbm_outs=[((leaves, width, columns), F32), ((1, width, columns), F32)],
        scratch=[
            pltpu.VMEM((leaves, width, columns), F32),
            pltpu.VMEM((width, columns), F32),
            pltpu.VMEM((depth, columns, width), BF16),
            pltpu.SMEM(pattern.shape, jnp.int32),
            pltpu.SemaphoreType.DMA,
            pltpu.SemaphoreType.DMA((leaves + 1,)),
        ],
    )


def local(
    leaf_right_hand,
    leaf_diagonal_inverse,
    leaf_coupling,
    leaf_pattern,
    top_rhs,
    top_inverse,
    top_coupling,
):
    depth = lax.axis_size("col").bit_length() - 1
    pattern = leaf_pattern.T

    own = own_factors(top_inverse, top_coupling)
    low, high, to_hub = chip_factors(own, swap(own, 1))
    factors = [None] * depth
    factors[depth - 1] = low
    factors[depth - 2] = high

    keep, send, cpl_last, forward, rounded = leaf_terms(
        True,
        pattern,
        leaf_coupling,
        (depth - 1,),
        top_rhs,
        leaf_right_hand,
        leaf_diagonal_inverse,
    )
    keep_rest, send_rest, cpl_rest = leaf_terms(
        False, pattern, leaf_coupling, tuple(range(depth - 1)), top_rhs, rounded=rounded
    )

    hub = swap(to_hub, 2)
    factors[depth - 3] = join_rows(hub, swap(hub, 1), "join_hub")
    spread = [swap(hub[: depth - 3], 4 | m << 3) for m in range(1 << (depth - 3))]
    for b in range(3, depth):
        level = depth - 1 - b
        part = pick(spread, b, level + 1, f"pick_{level}")
        factors[level] = join_rows(part, swap(part, 1), f"join_{level}")

    mine, theirs = keep, swap(send, 1)
    rest, their_rest = keep_rest, swap(send_rest, 1)
    forwards = [None] * depth
    for level in reversed(range(1, depth)):
        forwards[level], up = node_up(mine, theirs, factors[level], level)
        mine, *rest = add_terms(up, rest, their_rest)
        mask = 1 << (depth - level)
        theirs = swap(mine, mask)
        if rest:
            rest = rest[0]
            their_rest = swap(rest, mask)

    known = top_down(mine, theirs, forwards[1 : depth - 2], factors[: depth - 2])
    for level in (depth - 2, depth - 1):
        b = depth - level
        known = node_down(b, known, swap(known, 1 << b), forwards[level], factors[level])
    return leaf_down(
        pattern, known, swap(known, 1), forward, leaf_diagonal_inverse, [cpl_rest, cpl_last]
    )


def solution(mesh):
    in_specs = (
        P(("grp", "col"), None, None),
        P(("grp", "col"), None, None),
        P(("grp", "col"), None, None, None),
        P(("grp", "col"), None),
        P(("grp", "col"), None, None),
        P(("grp", "col"), None, None),
        P(("grp", "col"), None, None, None),
    )
    out_specs = (P(("grp", "col"), None, None), P(("grp", "col"), None, None))
    return jax.shard_map(local, mesh=mesh, in_specs=in_specs, out_specs=out_specs, check_vma=False)
```

time: 101 us -> 59 us (0.58)
  waiting for transfers between devices: 56.8 us -> 21.3 us
  Pallas kernels: 0 us -> 15 us
  matrix products: 14.8 us -> 0 us
  starting transfers between devices: 22.6 us -> 17.2 us
  other arithmetic: 1.92 us -> 0 us
  local copies, waits for them, and re-layouts: 3.17 us -> 4.45 us
    ppermute x20 -> x16, waiting for transfers between devices: 56.8 us -> 21.3 us  [swap(): return lax.ppermute(value, 'col', [(i, i ^ mask) for i in range(count)])]
    pallas_call x0 -> x17, Pallas kernels: none -> 15 us  [call(): pl.pallas_call(kernel, out_shape=tuple(shapes), in_specs=[ANY] * len(hbm_...]
    dot_general x14 -> x0, matrix products: 14.8 us -> none  [the longest x1 4.95 us: local(): jnp.einsum('vdu,vdo->vuo', leaf_diagonal_inverse, rounded_result(leaf_for...]
    ppermute x20 -> x16, starting transfers between devices: 22.6 us -> 17.2 us  [swap(): return lax.ppermute(value, 'col', [(i, i ^ mask) for i in range(count)])]
    unnamed x11 -> x14, local copies, waits for them, and re-layouts: 2.87 us -> 4.44 us
  transfers between devices with their start and end apart: 20 -> 16, of which waited for: 19 -> 9; matrix products, arithmetic and copies ran while one was open for 2% -> 0% of each run, Pallas kernels for 0% -> 16%
where the time goes in v2:
time: 59 us; the launch traced here: 58.8 us
  waiting for transfers between devices  21.3 us (36%)
  starting transfers between devices  17.2 us (29%)
  Pallas kernels  15 us (25%)
  local copies, waits for them, and re-layouts  4.45 us (8%)
  between operations  0.82 us (1%)
    ppermute x16, waiting for transfers between devices, swap(): return lax.ppermute(value, 'col', [(i, i ^ mask) for i in range(count)])  21.3 us
    ppermute x16, starting transfers between devices, swap(): return lax.ppermute(value, 'col', [(i, i ^ mask) for i in range(count)])  17.2 us
    pallas_call x17, Pallas kernels, call(): pl.pallas_call(kernel, out_shape=tuple(shapes), in_specs=[ANY] * len(hbm_...  15 us
    unnamed x14, local copies, waits for them, and re-layouts  4.44 us
  transfers between devices with their start and end apart: 16, of which 9 were waited for; matrix products, arithmetic and copies ran while one was open for 0% of the time, Pallas kernels for 16%

profile of v2, /device:TPU:0, one launch (start us, length us, event | category | flops | bytes accessed | tf_op | source)
XLA Modules:
  0.0 58.8 jit_solution(9089812846516008741)
XLA Ops:
  0.6 0.0 copy-start.4
  0.6 1.0 %copy-done.4 = bf16[1,4,256,256]{3,2,1,0:T(8,128)(2,1)S(1)} copy-done((bf16[1,4,256,256]{3,2,1,0:T(8,128)(2,1)S(1)}, bf16[1,4,256,256]{3,2,1,0:T(8,128)(2,1)}, u32[]{:S(2)}) %copy-start.4) | copy-done | bytes 524312
  1.7 0.0 copy-start.5
  1.7 0.9 %copy-done.5 = bf16[1,256,256]{2,1,0:T(8,128)(2,1)S(1)} copy-done((bf16[1,256,256]{2,1,0:T(8,128)(2,1)S(1)}, bf16[1,256,256]{2,1,0:T(8,128)(2,1)}, u32[]{:S(2)}) %copy-start.5) | copy-done | bytes 131096
  2.6 0.0 copy-start.2
  2.6 0.4 own_factors.1.own_ref
  3.0 0.0 copy-start.1
  3.0 0.0 copy-start.3
  3.0 0.0 copy-start.6
  3.0 0.6 collective-permute-start.1
  3.6 2.3 %collective-permute-done.1.other_ref = f32[4,256,256]{2,1,0:T(8,128)S(1)} collective-permute-done((f32[4,256,256]{2,1,0:T(8,128)S(1)}, f32[4,256,256]{2,1,0:T(8,128)S(1)}, u32[]{:S(2)}, u32[]{:S(2)}) %collective-permute-start.1) | collective-permute-done | bytes 1048608 | tf_op jit(solution)/shard_map/ppermute | solution.py:16
  5.9 0.1 chip_factors.1
  6.0 2.9 %collective-permute-start.6 = (f32[2,128,256]{2,1,0:T(8,128)S(1)}, f32[2,128,256]{2,1,0:T(8,128)S(1)}, u32[]{:S(2)}, u32[]{:S(2)}) collective-permute-start(f32[2,128,256]{2,1,0:T(8,128)S(1)} %get-tuple-element.35), channel_id=1, source_target_pairs={{0,2},{1,3},{2,0},{3,1},{4,6},{5,7},{6,4},{7,5},{8,10},{9,11},{10,... | collective-permute-start | bytes 786440 | tf_op jit(solution)/shard_map/ppermute | solution.py:16
  8.9 0.0 copy-done.2
  8.9 0.0 copy-done.1
  8.9 0.0 copy-done.3
  8.9 0.0 copy-done.6
  8.9 0.0 copy-start
  9.0 2.5 %copy-done = bf16[10,4,256,256]{3,2,1,0:T(8,128)(2,1)S(1)} copy-done((bf16[10,4,256,256]{3,2,1,0:T(8,128)(2,1)S(1)}, bf16[10,4,256,256]{3,2,1,0:T(8,128)(2,1)}, u32[]{:S(2)}) %copy-start) | copy-done | bytes 5242904
  11.4 3.7 %leaf_first.1 = (f32[1,64,256]{2,1,0:T(8,128)S(1)}, f32[1,64,256]{2,1,0:T(8,128)S(1)}, bf16[10,1,256,256]{3,2,1,0:T(8,128)(2,1)S(1)}, f32[10,128,256]{2,1,0:T(8,128)S(1)}, bf16[10,128,256]{2,1,0:T(8,128)(2,1)S(1)}) custom-call(s32[4,10]{1,0:T(4,128)S(1)} %bitcast.1, bf16[10,4,256,256]{3,2,1,0:T(8,128)(2,1)S(1)} %copy-done, f32[1,256,128]{2,1,0:T(8,128)S(1)} %copy-done.3, ...), custom_call_target="tpu_custom_call" | custom-call | flops 335544320 | bytes 5244064 | tf_op jit(solution)/shard_map/leaf_first/pallas_call | solution.py:40
  15.2 4.2 %leaf_rest.1 = (f32[3,64,256]{2,1,0:T(8,128)S(1)}, f32[3,64,256]{2,1,0:T(8,128)S(1)}, bf16[10,3,256,256]{3,2,1,0:T(8,128)(2,1)S(1)}) custom-call(s32[4,10]{1,0:T(4,128)S(1)} %bitcast.2, bf16[10,4,256,256]{3,2,1,0:T(8,128)(2,1)S(1)} %copy-done, f32[1,256,128]{2,1,0:T(8,128)S(1)} %copy-done.3, bf16[10,128,256]{2,1,0:T(8,128)(2,1)S(1)} %get-tuple-element.27.refs_0_), custom_call_target="tpu_custom_call" | custom-call | flops 503316480 | bytes 5244064 | tf_op jit(solution)/shard_map/leaf_rest/pallas_call | solution.py:40
  19.4 0.1 collective-permute-start.2
  19.5 0.5 collective-permute-start
  20.0 0.0 collective-permute-done.6.mine_ref
  20.0 0.1 collective-permute-start.7
  20.0 0.9 %collective-permute-done.theirs_ref = f32[1,64,256]{2,1,0:T(8,128)S(1)} collective-permute-done((f32[1,64,256]{2,1,0:T(8,128)S(1)}, f32[1,64,256]{2,1,0:T(8,128)S(1)}, u32[]{:S(2)}, u32[]{:S(2)}) %collective-permute-start) | collective-permute-done | bytes 65568 | tf_op jit(solution)/shard_map/ppermute | solution.py:16
  21.0 0.4 node_up_3.1
  21.4 0.0 collective-permute-done.2.theirs_ref
  21.4 0.1 collective-permute-start.4
  21.5 2.1 %collective-permute-start.10 = (f32[1,128,256]{2,1,0:T(8,128)S(1)}, f32[1,128,256]{2,1,0:T(8,128)S(1)}, u32[]{:S(2)}, u32[]{:S(2)}) collective-permute-start(f32[1,128,256]{2,1,0:T(8,128)S(1)} %slice.5), channel_id=1, source_target_pairs={{0,4},{1,5},{2,6},{3,7},{4,0},{5,1},{6,2},{7,3},{8,12},{9,13},{10,... | collective-permute-start | bytes 393224 | tf_op jit(solution)/shard_map/ppermute | solution.py:16
  23.7 2.5 %collective-permute-start.11 = (f32[1,128,256]{2,1,0:T(8,128)S(1)}, f32[1,128,256]{2,1,0:T(8,128)S(1)}, u32[]{:S(2)}, u32[]{:S(2)}) collective-permute-start(f32[1,128,256]{2,1,0:T(8,128)S(1)} %slice.5), channel_id=1, source_target_pairs={{0,12},{1,13},{2,14},{3,15},{4,8},{5,9},{6,10},{7,11},{8,4},{9,5},... | collective-permute-start | bytes 393224 | tf_op jit(solution)/shard_map/ppermute | solution.py:16
  26.1 1.5 %collective-permute-start.3 = (f32[1,64,256]{2,1,0:T(8,128)S(1)}, f32[1,64,256]{2,1,0:T(8,128)S(1)}, u32[]{:S(2)}, u32[]{:S(2)}) collective-permute-start(f32[1,64,256]{2,1,0:T(8,128)S(1)} %get-tuple-element.30.mine_ref), channel_id=1, source_target_pairs={{0,2},{1,3},{2,0},{3,1},{4,6},{5,7},{6,4},{7,5},{8,10},{9,11},{10,... | collective-permute-start | bytes 196616 | tf_op jit(solution)/shard_map/ppermute | solution.py:16
  27.7 2.7 %collective-permute-done.3.theirs_ref = f32[1,64,256]{2,1,0:T(8,128)S(1)} collective-permute-done((f32[1,64,256]{2,1,0:T(8,128)S(1)}, f32[1,64,256]{2,1,0:T(8,128)S(1)}, u32[]{:S(2)}, u32[]{:S(2)}) %collective-permute-start.3) | collective-permute-done | bytes 65568 | tf_op jit(solution)/shard_map/ppermute | solution.py:16
  30.4 0.4 node_up_2.1
  30.8 0.0 collective-permute-done.4.theirs_ref
  30.8 0.7 %collective-permute-start.5 = (f32[1,64,256]{2,1,0:T(8,128)S(1)}, f32[1,64,256]{2,1,0:T(8,128)S(1)}, u32[]{:S(2)}, u32[]{:S(2)}) collective-permute-start(f32[1,64,256]{2,1,0:T(8,128)S(1)} %get-tuple-element.34.mine_ref), channel_id=1, source_target_pairs={{0,4},{1,5},{2,6},{3,7},{4,0},{5,1},{6,2},{7,3},{8,12},{9,13},{10,... | collective-permute-start | bytes 196616 | tf_op jit(solution)/shard_map/ppermute | solution.py:16
  31.6 1.4 %collective-permute-start.8 = (f32[1,64,256]{2,1,0:T(8,128)S(1)}, f32[1,64,256]{2,1,0:T(8,128)S(1)}, u32[]{:S(2)}, u32[]{:S(2)}) collective-permute-start(f32[1,64,256]{2,1,0:T(8,128)S(1)} %get-tuple-element.37.mine_ref), channel_id=1, source_target_pairs={{0,4},{1,5},{2,6},{3,7},{4,0},{5,1},{6,2},{7,3},{8,12},{9,13},{10,... | collective-permute-start | bytes 196616 | tf_op jit(solution)/shard_map/ppermute | solution.py:16
  32.9 0.0 collective-permute-done.10.refs_0_
  32.9 0.0 collective-permute-done.11.refs_1_
  32.9 0.1 collective-permute-start.12
  33.0 0.0 collective-permute-done.7.other_ref
  33.1 2.1 %collective-permute-done.5.theirs_ref = f32[1,64,256]{2,1,0:T(8,128)S(1)} collective-permute-done((f32[1,64,256]{2,1,0:T(8,128)S(1)}, f32[1,64,256]{2,1,0:T(8,128)S(1)}, u32[]{:S(2)}, u32[]{:S(2)}) %collective-permute-start.5) | collective-permute-done | bytes 65568 | tf_op jit(solution)/shard_map/ppermute | solution.py:16
  35.2 0.3 node_up_1.1
  35.5 0.4 collective-permute-done.8.theirs_ref
  35.9 1.7 %collective-permute-start.9 = (f32[1,64,256]{2,1,0:T(8,128)S(1)}, f32[1,64,256]{2,1,0:T(8,128)S(1)}, u32[]{:S(2)}, u32[]{:S(2)}) collective-permute-start(f32[1,64,256]{2,1,0:T(8,128)S(1)} %add_terms_1.1.mine_ref), channel_id=1, source_target_pairs={{0,8},{1,9},{2,10},{3,11},{4,12},{5,13},{6,14},{7,15},{8,0},{9,1},... | collective-permute-start | bytes 196616 | tf_op jit(solution)/shard_map/ppermute | solution.py:16
  37.5 0.0 collective-permute-done.12.other_ref
  37.6 3.5 %collective-permute-done.9.theirs_ref = f32[1,64,256]{2,1,0:T(8,128)S(1)} collective-permute-done((f32[1,64,256]{2,1,0:T(8,128)S(1)}, f32[1,64,256]{2,1,0:T(8,128)S(1)}, u32[]{:S(2)}, u32[]{:S(2)}) %collective-permute-start.9) | collective-permute-done | bytes 65568 | tf_op jit(solution)/shard_map/ppermute | solution.py:16
  41.1 0.5 top_down.1.mine_ref
  41.6 1.4 %collective-permute-start.13 = (f32[2,64,256]{2,1,0:T(8,128)S(1)}, f32[2,64,256]{2,1,0:T(8,128)S(1)}, u32[]{:S(2)}, u32[]{:S(2)}) collective-permute-start(f32[2,64,256]{2,1,0:T(8,128)S(1)} %top_down.1.mine_ref), channel_id=1, source_target_pairs={{0,4},{1,5},{2,6},{3,7},{4,0},{5,1},{6,2},{7,3},{8,12},{9,13},{10,... | collective-permute-start | bytes 393224 | tf_op jit(solution)/shard_map/ppermute | solution.py:16
  43.0 3.6 %collective-permute-done.13.theirs_ref = f32[2,64,256]{2,1,0:T(8,128)S(1)} collective-permute-done((f32[2,64,256]{2,1,0:T(8,128)S(1)}, f32[2,64,256]{2,1,0:T(8,128)S(1)}, u32[]{:S(2)}, u32[]{:S(2)}) %collective-permute-start.13) | collective-permute-done | bytes 131104 | tf_op jit(solution)/shard_map/ppermute | solution.py:16
  46.7 0.3 node_down_2.1.mine_ref
  47.0 1.6 %collective-permute-start.14 = (f32[3,64,256]{2,1,0:T(8,128)S(1)}, f32[3,64,256]{2,1,0:T(8,128)S(1)}, u32[]{:S(2)}, u32[]{:S(2)}) collective-permute-start(f32[3,64,256]{2,1,0:T(8,128)S(1)} %node_down_2.1.mine_ref), channel_id=1, source_target_pairs={{0,2},{1,3},{2,0},{3,1},{4,6},{5,7},{6,4},{7,5},{8,10},{9,11},{10,... | collective-permute-start | bytes 589832 | tf_op jit(solution)/shard_map/ppermute | solution.py:16
  48.6 4.2 %collective-permute-done.14.theirs_ref = f32[3,64,256]{2,1,0:T(8,128)S(1)} collective-permute-done((f32[3,64,256]{2,1,0:T(8,128)S(1)}, f32[3,64,256]{2,1,0:T(8,128)S(1)}, u32[]{:S(2)}, u32[]{:S(2)}) %collective-permute-start.14) | collective-permute-done | bytes 196640 | tf_op jit(solution)/shard_map/ppermute | solution.py:16
  52.7 0.3 node_down_3.1.refs_0_
  53.1 0.1 collective-permute-start.15
  53.2 1.5 %collective-permute-done.15.refs_1_ = f32[4,64,256]{2,1,0:T(8,128)S(1)} collective-permute-done((f32[4,64,256]{2,1,0:T(8,128)S(1)}, f32[4,64,256]{2,1,0:T(8,128)S(1)}, u32[]{:S(2)}, u32[]{:S(2)}) %collective-permute-start.15) | collective-permute-done | bytes 262176 | tf_op jit(solution)/shard_map/ppermute | solution.py:16
  54.7 4.1 %leaf_down.1 = (f32[10,256,128]{2,1,0:T(8,128)}, f32[1,256,128]{2,1,0:T(8,128)}) custom-call(s32[4,10]{1,0:T(4,128)S(1)} %bitcast.3, f32[4,64,256]{2,1,0:T(8,128)S(1)} %node_down_3.1.refs_0_, f32[4,64,256]{2,1,0:T(8,128)S(1)} %collective-permute-done.15.refs_1_, f32[10,128,256]{2,1,0:T(8,128)S(1)} %get-tuple-element.41.refs_2_, ...), custom_call_target="tpu_custom_call" | custom-call | flops 838860800 | bytes 1184 | tf_op jit(solution)/shard_map/leaf_down/pallas_call | solution.py:40
  (7 shorter events, 0.2 us)
Async XLA Ops:
  0.6 1.0 %copy-start.4 = (bf16[1,4,256,256]{3,2,1,0:T(8,128)(2,1)S(1)}, bf16[1,4,256,256]{3,2,1,0:T(8,128)(2,1)}, u32[]{:S(2)}) copy-start(bf16[1,4,256,256]{3,2,1,0:T(8,128)(2,1)} %cpl_hbm.4) | copy-start | bytes 1572868
  1.7 0.9 %copy-start.5 = (bf16[1,256,256]{2,1,0:T(8,128)(2,1)S(1)}, bf16[1,256,256]{2,1,0:T(8,128)(2,1)}, u32[]{:S(2)}) copy-start(bf16[1,256,256]{2,1,0:T(8,128)(2,1)} %inv_hbm.1) | copy-start | bytes 393220
  2.6 6.4 %copy-start.2 = (f32[10,256,128]{2,1,0:T(8,128)S(1)}, f32[10,256,128]{2,1,0:T(8,128)}, u32[]{:S(2)}) copy-start(f32[10,256,128]{2,1,0:T(8,128)} %refs_0_.1) | copy-start | bytes 3932164
  3.0 5.9 %copy-start.1 = (bf16[10,256,256]{2,1,0:T(8,128)(2,1)S(1)}, bf16[10,256,256]{2,1,0:T(8,128)(2,1)}, u32[]{:S(2)}) copy-start(bf16[10,256,256]{2,1,0:T(8,128)(2,1)} %refs_3_.1) | copy-start | bytes 3932164
  3.0 5.9 %copy-start.3 = (f32[1,256,128]{2,1,0:T(8,128)S(1)}, f32[1,256,128]{2,1,0:T(8,128)}, u32[]{:S(2)}) copy-start(f32[1,256,128]{2,1,0:T(8,128)} %top_ref.3) | copy-start | bytes 393220
  3.0 5.9 %copy-start.6 = (s32[10,4]{0,1:T(4,128)S(1)}, s32[10,4]{0,1:T(4,128)}, u32[]{:S(2)}) copy-start(s32[10,4]{0,1:T(4,128)} %param.10) | copy-start | bytes 484
  3.0 2.8 %collective-permute-start.1 = (f32[4,256,256]{2,1,0:T(8,128)S(1)}, f32[4,256,256]{2,1,0:T(8,128)S(1)}, u32[]{:S(2)}, u32[]{:S(2)}) collective-permute-start(f32[4,256,256]{2,1,0:T(8,128)S(1)} %own_factors.1.own_ref), channel_id=1, source_target_pairs={{0,1},{1,0},{2,3},{3,2},{4,5},{5,4},{6,7},{7,6},{8,9},{9,8},{10,11... | collective-permute-start | bytes 3145736 | tf_op jit(solution)/shard_map/ppermute | solution.py:16
  6.0 14.0 %collective-permute-start.6 = (f32[2,128,256]{2,1,0:T(8,128)S(1)}, f32[2,128,256]{2,1,0:T(8,128)S(1)}, u32[]{:S(2)}, u32[]{:S(2)}) collective-permute-start(f32[2,128,256]{2,1,0:T(8,128)S(1)} %get-tuple-element.35), channel_id=1, source_target_pairs={{0,2},{1,3},{2,0},{3,1},{4,6},{5,7},{6,4},{7,5},{8,10},{9,11},{10,... | collective-permute-start | bytes 786440 | tf_op jit(solution)/shard_map/ppermute | solution.py:16
  8.9 2.5 %copy-start = (bf16[10,4,256,256]{3,2,1,0:T(8,128)(2,1)S(1)}, bf16[10,4,256,256]{3,2,1,0:T(8,128)(2,1)}, u32[]{:S(2)}) copy-start(bf16[10,4,256,256]{3,2,1,0:T(8,128)(2,1)} %cpl_hbm.5) | copy-start | bytes 15728644
  19.4 2.0 %collective-permute-start.2 = (f32[3,64,256]{2,1,0:T(8,128)S(1)}, f32[3,64,256]{2,1,0:T(8,128)S(1)}, u32[]{:S(2)}, u32[]{:S(2)}) collective-permute-start(f32[3,64,256]{2,1,0:T(8,128)S(1)} %get-tuple-element.29), channel_id=1, source_target_pairs={{0,1},{1,0},{2,3},{3,2},{4,5},{5,4},{6,7},{7,6},{8,9},{9,8},{10,11... | collective-permute-start | bytes 589832 | tf_op jit(solution)/shard_map/ppermute | solution.py:16
  19.5 1.5 %collective-permute-start = (f32[1,64,256]{2,1,0:T(8,128)S(1)}, f32[1,64,256]{2,1,0:T(8,128)S(1)}, u32[]{:S(2)}, u32[]{:S(2)}) collective-permute-start(f32[1,64,256]{2,1,0:T(8,128)S(1)} %get-tuple-element.24), channel_id=1, source_target_pairs={{0,1},{1,0},{2,3},{3,2},{4,5},{5,4},{6,7},{7,6},{8,9},{9,8},{10,11... | collective-permute-start | bytes 196616 | tf_op jit(solution)/shard_map/ppermute | solution.py:16
  20.0 13.1 %collective-permute-start.7 = (f32[2,128,256]{2,1,0:T(8,128)S(1)}, f32[2,128,256]{2,1,0:T(8,128)S(1)}, u32[]{:S(2)}, u32[]{:S(2)}) collective-permute-start(f32[2,128,256]{2,1,0:T(8,128)S(1)} %collective-permute-done.6.mine_ref), channel_id=1, source_target_pairs={{0,1},{1,0},{2,3},{3,2},{4,5},{5,4},{6,7},{7,6},{8,9},{9,8},{10,11... | collective-permute-start | bytes 786440 | tf_op jit(solution)/shard_map/ppermute | solution.py:16
  21.4 9.3 %collective-permute-start.4 = (f32[2,64,256]{2,1,0:T(8,128)S(1)}, f32[2,64,256]{2,1,0:T(8,128)S(1)}, u32[]{:S(2)}, u32[]{:S(2)}) collective-permute-start(f32[2,64,256]{2,1,0:T(8,128)S(1)} %get-tuple-element.33.mine_ref), channel_id=1, source_target_pairs={{0,2},{1,3},{2,0},{3,1},{4,6},{5,7},{6,4},{7,5},{8,10},{9,11},{10,... | collective-permute-start | bytes 393224 | tf_op jit(solution)/shard_map/ppermute | solution.py:16
  21.5 11.4 %collective-permute-start.10 = (f32[1,128,256]{2,1,0:T(8,128)S(1)}, f32[1,128,256]{2,1,0:T(8,128)S(1)}, u32[]{:S(2)}, u32[]{:S(2)}) collective-permute-start(f32[1,128,256]{2,1,0:T(8,128)S(1)} %slice.5), channel_id=1, source_target_pairs={{0,4},{1,5},{2,6},{3,7},{4,0},{5,1},{6,2},{7,3},{8,12},{9,13},{10,... | collective-permute-start | bytes 393224 | tf_op jit(solution)/shard_map/ppermute | solution.py:16
  23.7 9.3 %collective-permute-start.11 = (f32[1,128,256]{2,1,0:T(8,128)S(1)}, f32[1,128,256]{2,1,0:T(8,128)S(1)}, u32[]{:S(2)}, u32[]{:S(2)}) collective-permute-start(f32[1,128,256]{2,1,0:T(8,128)S(1)} %slice.5), channel_id=1, source_target_pairs={{0,12},{1,13},{2,14},{3,15},{4,8},{5,9},{6,10},{7,11},{8,4},{9,5},... | collective-permute-start | bytes 393224 | tf_op jit(solution)/shard_map/ppermute | solution.py:16
  26.1 4.3 %collective-permute-start.3 = (f32[1,64,256]{2,1,0:T(8,128)S(1)}, f32[1,64,256]{2,1,0:T(8,128)S(1)}, u32[]{:S(2)}, u32[]{:S(2)}) collective-permute-start(f32[1,64,256]{2,1,0:T(8,128)S(1)} %get-tuple-element.30.mine_ref), channel_id=1, source_target_pairs={{0,2},{1,3},{2,0},{3,1},{4,6},{5,7},{6,4},{7,5},{8,10},{9,11},{10,... | collective-permute-start | bytes 196616 | tf_op jit(solution)/shard_map/ppermute | solution.py:16
  30.8 4.3 %collective-permute-start.5 = (f32[1,64,256]{2,1,0:T(8,128)S(1)}, f32[1,64,256]{2,1,0:T(8,128)S(1)}, u32[]{:S(2)}, u32[]{:S(2)}) collective-permute-start(f32[1,64,256]{2,1,0:T(8,128)S(1)} %get-tuple-element.34.mine_ref), channel_id=1, source_target_pairs={{0,4},{1,5},{2,6},{3,7},{4,0},{5,1},{6,2},{7,3},{8,12},{9,13},{10,... | collective-permute-start | bytes 196616 | tf_op jit(solution)/shard_map/ppermute | solution.py:16
  31.6 4.3 %collective-permute-start.8 = (f32[1,64,256]{2,1,0:T(8,128)S(1)}, f32[1,64,256]{2,1,0:T(8,128)S(1)}, u32[]{:S(2)}, u32[]{:S(2)}) collective-permute-start(f32[1,64,256]{2,1,0:T(8,128)S(1)} %get-tuple-element.37.mine_ref), channel_id=1, source_target_pairs={{0,4},{1,5},{2,6},{3,7},{4,0},{5,1},{6,2},{7,3},{8,12},{9,13},{10,... | collective-permute-start | bytes 196616 | tf_op jit(solution)/shard_map/ppermute | solution.py:16
  32.9 4.6 %collective-permute-start.12 = (f32[1,128,256]{2,1,0:T(8,128)S(1)}, f32[1,128,256]{2,1,0:T(8,128)S(1)}, u32[]{:S(2)}, u32[]{:S(2)}) collective-permute-start(f32[1,128,256]{2,1,0:T(8,128)S(1)} %pick_0.1.mine_ref), channel_id=1, source_target_pairs={{0,1},{1,0},{2,3},{3,2},{4,5},{5,4},{6,7},{7,6},{8,9},{9,8},{10,11... | collective-permute-start | bytes 393224 | tf_op jit(solution)/shard_map/ppermute | solution.py:16
  35.9 5.2 %collective-permute-start.9 = (f32[1,64,256]{2,1,0:T(8,128)S(1)}, f32[1,64,256]{2,1,0:T(8,128)S(1)}, u32[]{:S(2)}, u32[]{:S(2)}) collective-permute-start(f32[1,64,256]{2,1,0:T(8,128)S(1)} %add_terms_1.1.mine_ref), channel_id=1, source_target_pairs={{0,8},{1,9},{2,10},{3,11},{4,12},{5,13},{6,14},{7,15},{8,0},{9,1},... | collective-permute-start | bytes 196616 | tf_op jit(solution)/shard_map/ppermute | solution.py:16
  41.6 5.0 %collective-permute-start.13 = (f32[2,64,256]{2,1,0:T(8,128)S(1)}, f32[2,64,256]{2,1,0:T(8,128)S(1)}, u32[]{:S(2)}, u32[]{:S(2)}) collective-permute-start(f32[2,64,256]{2,1,0:T(8,128)S(1)} %top_down.1.mine_ref), channel_id=1, source_target_pairs={{0,4},{1,5},{2,6},{3,7},{4,0},{5,1},{6,2},{7,3},{8,12},{9,13},{10,... | collective-permute-start | bytes 393224 | tf_op jit(solution)/shard_map/ppermute | solution.py:16
  47.0 5.7 %collective-permute-start.14 = (f32[3,64,256]{2,1,0:T(8,128)S(1)}, f32[3,64,256]{2,1,0:T(8,128)S(1)}, u32[]{:S(2)}, u32[]{:S(2)}) collective-permute-start(f32[3,64,256]{2,1,0:T(8,128)S(1)} %node_down_2.1.mine_ref), channel_id=1, source_target_pairs={{0,2},{1,3},{2,0},{3,1},{4,6},{5,7},{6,4},{7,5},{8,10},{9,11},{10,... | collective-permute-start | bytes 589832 | tf_op jit(solution)/shard_map/ppermute | solution.py:16
  53.1 1.6 %collective-permute-start.15 = (f32[4,64,256]{2,1,0:T(8,128)S(1)}, f32[4,64,256]{2,1,0:T(8,128)S(1)}, u32[]{:S(2)}, u32[]{:S(2)}) collective-permute-start(f32[4,64,256]{2,1,0:T(8,128)S(1)} %node_down_3.1.refs_0_), channel_id=1, source_target_pairs={{0,1},{1,0},{2,3},{3,2},{4,5},{5,4},{6,7},{7,6},{8,9},{9,8},{10,11... | collective-permute-start | bytes 786440 | tf_op jit(solution)/shard_map/ppermute | solution.py:16
